TPU v7x, 32 devices: a whole 2x2x4 slice. The times are simulated.
32 devices in a mesh: grp: 2 (over y), bin: 4 (over z), slab: 4 (over x, core).
Axes of the slice: x: 2, y: 2, z: 4, core: 2. Of those that a mesh axis runs over, the one named last changes fastest.
Arguments:
- density: bfloat16 [512, 256, 256], P('grp', 'slab'), parts along dimension 0, may hold values from -6 to 6
- images: bfloat16 [512, 128, 128], P(('grp', 'bin', 'slab')), parts along dimension 0, may hold values from -6 to 6
- image_bin: int32 [512, 1], P(('grp', 'bin', 'slab')), parts along dimension 0, may hold values from 0 to 3; in each aligned block of 16 rows (0 to 15, 16 to 31, ...) at most 4 rows name the same one
- image_pose: int32 [512], P(('grp', 'bin', 'slab')), parts along dimension 0, may hold values from 0 to 7
- image_class: int32 [512], P(('grp', 'bin', 'slab')), parts along dimension 0, may hold values from 0 to 15
- defocus: float32 [32], P('grp'), parts along dimension 0, may hold values from 1 to 3
- pose_offset: float32 [8, 8], P('grp'), parts along dimension 0, may hold values from 0 to 1
- step_sizes: float32 [2], replicated, may hold values from 0.2 to 0.8
Outputs:
- gradient: float32 [512, 256, 256], P(('grp', 'bin'), 'slab'), parts along dimension 0
- refined: float32 [512, 256, 256], P(('grp', 'bin'), 'slab'), parts along dimension 0
There are 2 independent parts, one for each index of `grp`. A program takes and returns all parts, laid end to end along the dimension named above; an argument that names none is the same for every part. Nothing has to cross between parts.
Inputs may be any that keep to these rules, and one draw needn't show every extreme that they name: `image_bin`: the images of one device name each bin at most 4 times, a bound that some block reaches.
All inputs are finite; a program needn't handle non-finite values.
Results may differ from a plain program's by a relative error of at most 0.0032.
Values may be sent and summed in bfloat16 or wider, within the bound.
No kernel may reach another device: no remote copies, remote signals or barrier semaphores. Data moves between devices by JAX's collectives and lax.ppermute only.
A program may use at most 256 MiB of HBM per device.

v0:
```python
import math

import jax
import jax.numpy as jnp
from jax import lax
from jax.sharding import PartitionSpec as P

AMP_CONTRAST = 0.1
PHASE_RATE = 60.0
PRECISE = lax.Precision.HIGHEST


def pool_table(image_side, map_side):
    row_index = jnp.arange(image_side, dtype=jnp.float32)[:, None]
    col_index = jnp.arange(map_side, dtype=jnp.float32)[None, :]
    return 0.5 * jnp.maximum(0.0, 1.0 - jnp.abs(col_index - 2.0 * row_index - 0.5) / 2.0)


def slice_weights(angle_value, image_side, map_side, first_plane, slab_depth):
    middle = map_side / 2.0
    y_coord = jnp.arange(map_side, dtype=jnp.float32)[:, None] + 0.5 - middle
    z_coord = (
        (first_plane + jnp.arange(slab_depth, dtype=jnp.int32)).astype(jnp.float32)[None, :]
        + 0.5
        - middle
    )
    spot_line = (y_coord * jnp.cos(angle_value) + z_coord * jnp.sin(angle_value)).reshape(
        1, map_side * slab_depth
    )
    centre = 2.0 * jnp.arange(image_side, dtype=jnp.float32)[:, None] + 1.0 - middle
    factor = 0.5 / math.sqrt(map_side)
    return (factor * jnp.maximum(0.0, 1.0 - jnp.abs(spot_line - centre) / 2.0)).astype(jnp.bfloat16)


def ctf_of(defocus_value, image_side):
    index_row = jnp.arange(image_side, dtype=jnp.int32)
    frequency = (
        jnp.where(index_row < image_side // 2, index_row, index_row - image_side).astype(
            jnp.float32
        )
        / image_side
    )
    radius = frequency[:, None] * frequency[:, None] + frequency[None, :] * frequency[None, :]
    phase_shift = PHASE_RATE * defocus_value[:, None, None] * radius[None, :, :]
    return -(
        math.sqrt(1.0 - AMP_CONTRAST * AMP_CONTRAST) * jnp.sin(phase_shift)
        + AMP_CONTRAST * jnp.cos(phase_shift)
    )


def dft_tables(image_side):
    index_row = jnp.arange(image_side, dtype=jnp.int32)
    phase_index = index_row[:, None] * index_row[None, :] % image_side
    angle_table = 2.0 * math.pi / image_side * phase_index.astype(jnp.float32)
    factor = 1.0 / math.sqrt(image_side)
    return (jnp.cos(angle_table) * factor, jnp.sin(angle_table) * factor)


def forward(grid, cosine, sine_table):
    along_cos = jnp.einsum("bmn,nk->bmk", grid, cosine, precision=PRECISE)
    along_sin = jnp.einsum("bmn,nk->bmk", grid, sine_table, precision=PRECISE)
    real_part = jnp.einsum("lm,bmk->blk", cosine, along_cos, precision=PRECISE) - jnp.einsum(
        "lm,bmk->blk", sine_table, along_sin, precision=PRECISE
    )
    imag_part = -(
        jnp.einsum("lm,bmk->blk", sine_table, along_cos, precision=PRECISE)
        + jnp.einsum("lm,bmk->blk", cosine, along_sin, precision=PRECISE)
    )
    return (real_part, imag_part)


def inverse_real(real_part, imag_part, cosine, sine_table):
    inner_real = jnp.einsum("blk,kn->bln", real_part, cosine, precision=PRECISE) - jnp.einsum(
        "blk,kn->bln", imag_part, sine_table, precision=PRECISE
    )
    inner_imag = jnp.einsum("blk,kn->bln", imag_part, cosine, precision=PRECISE) + jnp.einsum(
        "blk,kn->bln", real_part, sine_table, precision=PRECISE
    )
    return jnp.einsum("ml,bln->bmn", cosine, inner_real, precision=PRECISE) - jnp.einsum(
        "ml,bln->bmn", sine_table, inner_imag, precision=PRECISE
    )


def on_device(
    density, images, image_bin, image_pose, image_class, defocus, pose_offset, step_sizes
):
    bin_count = lax.axis_size("bin")
    slab_count = lax.axis_size("slab")
    bin_index = lax.axis_index("bin")
    slab_index = lax.axis_index("slab")
    map_side, slab_depth, _ = density.shape
    image_count, image_side, _ = images.shape
    pose_count = pose_offset.shape[1]
    class_count = defocus.shape[0]
    capacity = image_count // 4
    slot_count = bin_count * capacity
    pixel_count = image_side * image_side
    row_share = map_side // bin_count
    weight = 16.0 * pose_count / (image_count * slab_count)
    pooling = pool_table(image_side, map_side)
    pool_half = pooling.astype(jnp.bfloat16)
    cosine, sine_table = dft_tables(image_side)
    offset_row = lax.dynamic_index_in_dim(pose_offset, bin_index, 0, keepdims=False)
    angles = math.pi * (bin_index.astype(jnp.float32) + offset_row) / bin_count

    def make_slice(angle_value):
        return slice_weights(angle_value, image_side, map_side, slab_index * slab_depth, slab_depth)

    slices = lax.map(make_slice, angles)
    target = image_bin[:, 0]
    chosen = (target[:, None] == jnp.arange(bin_count, dtype=jnp.int32)[None, :]).astype(jnp.int32)
    earlier = jnp.cumsum(chosen, axis=0) - chosen
    order_rank = jnp.sum(earlier * chosen, axis=1)
    slot_index = target * capacity + order_rank
    placement = jnp.arange(slot_count, dtype=jnp.int32)[:, None] == slot_index[None, :]
    sent_pixels = jnp.dot(
        placement.astype(jnp.bfloat16),
        images.reshape(image_count, pixel_count),
        preferred_element_type=jnp.float32,
    ).astype(jnp.bfloat16)
    label_pairs = jnp.stack([image_pose + 1, image_class + 1], axis=1)
    sent_labels = jnp.dot(placement.astype(jnp.int32), label_pairs) - 1
    got_pixels, got_labels = (
        lax.all_to_all(
            sent_pixels.reshape(bin_count, capacity, pixel_count),
            "bin",
            split_axis=0,
            concat_axis=0,
            tiled=True,
        ),
        lax.all_to_all(
            sent_labels.reshape(bin_count, capacity, 2),
            "bin",
            split_axis=0,
            concat_axis=0,
            tiled=True,
        ),
    )
    grid = got_pixels.astype(jnp.float32).reshape(slot_count, image_side, image_side)
    fourier_real, fourier_imag = forward(grid, cosine, sine_table)
    fourier_real = fourier_real.reshape(slot_count, pixel_count)
    fourier_imag = fourier_imag.reshape(slot_count, pixel_count)
    arrived = got_labels.reshape(slot_count, 2)
    pose_hot = (arrived[:, 0:1] == jnp.arange(pose_count, dtype=jnp.int32)[None, :]).astype(
        jnp.float32
    )
    class_hot = (arrived[:, 1:2] == jnp.arange(class_count, dtype=jnp.int32)[None, :]).astype(
        jnp.float32
    )
    slot_defocus = jnp.sum(class_hot * defocus[None, :], axis=1)
    ctf = ctf_of(slot_defocus, image_side).reshape(slot_count, pixel_count)

    def fold_rows(block_rows):
        folded = jnp.einsum(
            "yzx,ix->yzi", block_rows, pool_half, preferred_element_type=jnp.float32
        )
        return folded.astype(jnp.bfloat16)

    def back_project(folded):
        flat_folded = folded.reshape(map_side * slab_depth, image_side)
        partial_value = jnp.einsum(
            "pjk,ki->pij", slices, flat_folded, preferred_element_type=jnp.float32
        )
        projection = lax.psum(partial_value, "slab")
        model_real, model_imag = forward(projection, cosine, sine_table)
        model_real = model_real.reshape(pose_count, pixel_count)
        model_imag = model_imag.reshape(pose_count, pixel_count)
        look_real = jnp.dot(pose_hot, model_real, precision=PRECISE)
        look_imag = jnp.dot(pose_hot, model_imag, precision=PRECISE)
        term_real = ctf * (ctf * look_real - fourier_real)
        term_imag = ctf * (ctf * look_imag - fourier_imag)
        sum_real = weight * jnp.dot(pose_hot.T, term_real, precision=PRECISE)
        sum_imag = weight * jnp.dot(pose_hot.T, term_imag, precision=PRECISE)
        sheets = inverse_real(
            sum_real.reshape(pose_count, image_side, image_side),
            sum_imag.reshape(pose_count, image_side, image_side),
            cosine,
            sine_table,
        )
        sheets = lax.psum(sheets, "slab").astype(jnp.bfloat16)
        return jnp.einsum("pjk,pij->ki", slices, sheets, preferred_element_type=jnp.float32)

    def spread(back):
        result = jnp.dot(back, pooling, precision=PRECISE)
        return lax.psum_scatter(
            result.reshape(row_share * lax.axis_size("bin"), slab_depth, map_side),
            "bin",
            scatter_dimension=0,
            tiled=True,
        )

    gradient_first = spread(back_project(fold_rows(density)))
    own_rows = lax.dynamic_slice_in_dim(density, bin_index * row_share, row_share, 0).astype(
        jnp.float32
    )
    first = own_rows - step_sizes[0] * gradient_first
    folded_next = fold_rows(lax.all_gather(first.astype(jnp.bfloat16), "bin", axis=0, tiled=True))
    gradient = spread(back_project(folded_next))
    refined = first - step_sizes[1] * gradient
    return (gradient, refined)


def solution(mesh):
    return jax.shard_map(
        on_device,
        mesh=mesh,
        in_specs=(
            P("grp", "slab", None),
            P(("grp", "bin", "slab"), None, None),
            P(("grp", "bin", "slab"), None),
            P(("grp", "bin", "slab")),
            P(("grp", "bin", "slab")),
            P("grp"),
            P("grp", None),
            P(),
        ),
        out_specs=(P(("grp", "bin"), "slab", None), P(("grp", "bin"), "slab", None)),
        check_vma=False,
    )
```

profile of v0, /device:TPU:0, one launch (start us, length us, event | category | flops | bytes accessed | tf_op | source)
XLA Modules:
  0.0 1119.6 jit_solution(18046282025647319647)
XLA Ops:
  7.9 46.4 %while.15 = (s32[]{:T(128)}, bf16[8,128,16384]{2,1,0:T(8,128)(2,1)}, f32[8]{0:T(128)S(1)}, s32[]{:T(128)}, s32[]{:T(128)}) while((s32[]{:T(128)}, bf16[8,128,16384]{2,1,0:T(8,128)(2,1)}, f32[8]{0:T(128)S(1)}, s32[]{:T(128)}, s32[]{:T(128)}) %tuple.48), condition=%wide.region_1.2_spmd, body=%wide.region_0.1_spmd.sunk | while | flops 14697474 | bytes 4460645 | solution.py:109
  10.0 3.8 fusion.347
  15.7 3.8 fusion.347
  21.6 3.8 fusion.347
  27.4 3.8 fusion.347
  33.2 3.8 fusion.347
  39.0 3.8 fusion.347
  44.8 3.8 fusion.347
  50.6 3.8 fusion.347
  54.3 10.8 convert_bitcast_fusion
  65.1 6.4 copy.105
  71.6 17.7 %convolution_bitcast_fusion.3 = f32[8,128,128]{2,1,0:T(8,128)} fusion(bf16[16384,128,1]{1,0,2:T(8,128)(2,1)} %bitcast.202, bf16[8,128,16384]{2,1,0:T(8,128)(2,1)} %get-tuple-element.111), kind=kOutput, calls=%fused_computation.60 | convolution fusion | flops 4294967296 | bytes 38273024 | tf_op jit(solution)/shard_map/pjk,ki->pij/dot_general | solution.py:161
  90.5 6.3 all-to-all-start
  97.5 1.0 reshape.261
  98.5 4.0 all-to-all-done
  102.4 3.5 all-to-all-start.1
  106.7 18.9 %all-reduce.5.cloned.1.call-done = f32[8,128,128]{2,1,0:T(8,128)} async-done(((f32[8,128,128]{2,1,0:T(8,128)}), f32[8,128,128]{2,1,0:T(8,128)}) %all-reduce.5.cloned.1.call-update) | async-done | bytes 524304 | tf_op jit(solution)/shard_map/psum | solution.py:164
  125.6 1.9 fusion.102
  127.5 0.8 fusion.73
  128.4 1.9 fusion.79
  130.3 0.8 fusion.23
  131.3 0.8 fusion.100
  133.0 1.0 copy.109
  134.5 0.8 fusion.98
  135.4 0.8 fusion.76
  136.2 1.2 fusion.71
  137.5 1.2 fusion.96
  138.7 2.2 fusion.11
  140.9 2.5 copy.119
  143.4 6.4 fusion.6
  151.2 2.2 fusion.12
  153.4 1.6 copy.112
  155.0 6.1 fusion.8
  163.3 0.8 convolution_subtract_fusion.5
  164.2 1.1 fusion.91
  165.3 1.1 fusion.21
  166.4 16.5 %all-reduce.8 = bf16[8,128,128]{1,2,0:T(8,128)(2,1)S(1)} all-reduce(f32[8,128,128]{1,2,0:T(8,128)S(1)} %fusion.21), channel_id=1, replica_groups=mesh['grp'=2,'bin'=4,'slab'=4] {'slab'}, use_global_device_ids=true, to_apply=%region_6.7 | all-reduce | flops 131072 | bytes 786432 | tf_op jit(solution)/shard_map/psum | solution.py:180
  182.9 14.8 %convolution_bitcast_fusion.1 = f32[16384,128]{1,0:T(8,128)S(1)} fusion(bf16[8,128,16384]{2,1,0:T(8,128)(2,1)} %get-tuple-element.111, bf16[8,128,128]{1,2,0:T(8,128)(2,1)S(1)} %all-reduce.8), kind=kOutput, calls=%fused_computation.7 | convolution fusion | flops 4294967296 | bytes 42205184 | tf_op jit(solution)/shard_map/pjk,pij->ki/dot_general | solution.py:181
  197.7 14.0 %fusion.54 = f32[16384,256]{1,0:T(8,128)S(1)} fusion(f32[16384,128]{1,0:T(8,128)S(1)} %convolution_bitcast_fusion.1, f32[128]{0:T(128)S(1)} %iota_multiply_fusion), kind=kOutput, calls=%fused_computation.92 | convolution fusion | flops 6442680320 | bytes 25166336 | tf_op jit(solution)/shard_map/dot_general | solution.py:184
  211.7 19.7 %copy.127 = f32[256,64,256]{2,0,1:T(8,128)} copy(f32[256,64,256]{2,1,0:T(8,128)S(1)} %bitcast.201) | data formatting | bytes 33554432 | tf_op jit(solution)/shard_map/reshape | solution.py:186
  231.5 11.4 %copy.103 = bf16[256,64,256]{2,0,1:T(8,128)(2,1)} copy(bf16[256,64,256]{2,1,0:T(8,128)(2,1)} %param.10) | data formatting | bytes 16777216 | tf_op args[0]
  243.5 268.7 %reduce-scatter.3.cloned.1.call-done = f32[64,64,256]{2,0,1:T(8,128)} async-done(((f32[256,64,256]{2,0,1:T(8,128)}), f32[64,64,256]{2,0,1:T(8,128)}) %reduce-scatter.3.cloned.1.call-update) | async-done | bytes 4194320 | tf_op jit(solution)/shard_map/reduce_scatter | solution.py:185
  512.2 5.6 fusion.9
  518.0 150.1 %all-gather.2.cloned.1.call-done = bf16[256,64,256]{2,0,1:T(8,128)(2,1)} async-done(((bf16[64,64,256]{2,0,1:T(8,128)(2,1)}), bf16[256,64,256]{2,0,1:T(8,128)(2,1)}) %all-gather.2.cloned.1.call-update) | async-done | bytes 8388624 | tf_op jit(solution)/shard_map/all_gather | solution.py:197
  668.1 5.8 convolution_convert_fusion.1
  673.9 2.7 copy.128
  676.7 16.9 %convolution_bitcast_fusion.2 = f32[8,128,128]{2,1,0:T(8,128)} fusion(bf16[16384,128,1]{1,0,2:T(8,128)(2,1)S(1)} %bitcast.203, bf16[8,128,16384]{2,1,0:T(8,128)(2,1)} %get-tuple-element.111), kind=kOutput, calls=%fused_computation.59 | convolution fusion | flops 4294967296 | bytes 38273024 | tf_op jit(solution)/shard_map/pjk,ki->pij/dot_general | solution.py:161
  693.9 31.5 %all-reduce.7.cloned.1.call-done = f32[8,128,128]{2,1,0:T(8,128)} async-done(((f32[8,128,128]{2,1,0:T(8,128)}), f32[8,128,128]{2,1,0:T(8,128)}) %all-reduce.7.cloned.1.call-update) | async-done | bytes 524304 | tf_op jit(solution)/shard_map/psum | solution.py:164
  725.4 1.9 fusion.88
  727.3 0.8 fusion.63
  729.0 1.9 fusion.66
  730.9 0.8 fusion.19
  731.9 4.8 fusion.2
  739.1 6.5 fusion.4
  748.7 1.1 fusion.82
  749.8 1.1 fusion.17
  751.0 16.7 %all-reduce.9 = bf16[8,128,128]{1,2,0:T(8,128)(2,1)S(1)} all-reduce(f32[8,128,128]{1,2,0:T(8,128)S(1)} %fusion.17), channel_id=1, replica_groups=mesh['grp'=2,'bin'=4,'slab'=4] {'slab'}, use_global_device_ids=true, to_apply=%region_9.10 | all-reduce | flops 131072 | bytes 786432 | tf_op jit(solution)/shard_map/psum | solution.py:180
  767.7 14.8 %convolution_bitcast_fusion = f32[16384,128]{1,0:T(8,128)S(1)} fusion(bf16[8,128,16384]{2,1,0:T(8,128)(2,1)} %get-tuple-element.111, bf16[8,128,128]{1,2,0:T(8,128)(2,1)S(1)} %all-reduce.9), kind=kOutput, calls=%fused_computation.6 | convolution fusion | flops 4294967296 | bytes 42205184 | tf_op jit(solution)/shard_map/pjk,pij->ki/dot_general | solution.py:181
  782.5 14.0 %fusion.53 = f32[16384,256]{1,0:T(8,128)S(1)} fusion(f32[16384,128]{1,0:T(8,128)S(1)} %convolution_bitcast_fusion, f32[128]{0:T(128)S(1)} %iota_multiply_fusion), kind=kOutput, calls=%fused_computation.91 | convolution fusion | flops 6442680320 | bytes 25166336 | tf_op jit(solution)/shard_map/dot_general | solution.py:184
  796.5 19.5 %copy.144 = f32[256,64,256]{2,0,1:T(8,128)} copy(f32[256,64,256]{2,1,0:T(8,128)S(1)} %bitcast.200) | data formatting | bytes 33554432 | tf_op jit(solution)/shard_map/reshape | solution.py:186
  816.0 280.9 %reduce-scatter.5.cloned.1.call-done = f32[64,64,256]{2,0,1:T(8,128)} async-done(((f32[256,64,256]{2,0,1:T(8,128)}), f32[64,64,256]{2,0,1:T(8,128)}) %reduce-scatter.5.cloned.1.call-update) | async-done | bytes 4194320 | tf_op jit(solution)/shard_map/reduce_scatter | solution.py:185
  1096.9 7.1 multiply_subtract_fusion
  1104.0 4.4 copy.146
  1108.4 4.4 copy.145
  (116 shorter events, 22.0 us)
Async XLA Ops:
  7.2 118.5 %all-reduce.5.cloned.1.call-start = ((), (), s32[]{:S(2)}) async-start(), calls=%async_computation.4 | async-start | bytes 1048576 | tf_op jit(solution)/shard_map/psum | solution.py:164
  71.6 17.8 %copy-start.4 = (s32[16,1]{0,1:T(1,128)S(1)}, s32[16,1]{0,1:T(1,128)}, u32[]{:S(2)}) copy-start(s32[16,1]{0,1:T(1,128)} %param.12) | copy-start | bytes 196
  71.6 18.1 %copy-start.6 = (s32[16]{0:T(128)S(1)}, s32[16]{0:T(128)}, u32[]{:S(2)}) copy-start(s32[16]{0:T(128)} %param.14) | copy-start | bytes 196
  71.6 18.1 %copy-start.7 = (s32[16]{0:T(128)S(1)}, s32[16]{0:T(128)}, u32[]{:S(2)}) copy-start(s32[16]{0:T(128)} %param.13) | copy-start | bytes 196
  71.6 25.5 %copy-start.3 = (bf16[16,128,128]{2,1,0:T(8,128)(2,1)S(1)}, bf16[16,128,128]{2,1,0:T(8,128)(2,1)}, u32[]{:S(2)}) copy-start(bf16[16,128,128]{2,1,0:T(8,128)(2,1)} %param.11) | copy-start | bytes 1572868
  71.6 34.9 %copy-start.8 = (f32[16]{0:T(128)S(1)}, f32[16]{0:T(128)}, u32[]{:S(2)}) copy-start(f32[16]{0:T(128)} %param.15) | copy-start | bytes 196
  90.5 11.9 %all-to-all-start = ((s32[4,4,2]{1,2,0:T(2,128)}), s32[4,4,2]{1,2,0:T(2,128)S(1)}, u32[]{:S(2)}, u32[]{:S(2)}) async-start(s32[4,4,2]{1,2,0:T(2,128)} %copy.101), calls=%async_computation | async-start | bytes 8192 | tf_op jit(solution)/shard_map/all_to_all | solution.py:131
  102.4 31.6 %all-to-all-start.1 = ((bf16[4,4,16384]{2,1,0:T(4,128)(2,1)}), bf16[4,4,16384]{2,1,0:T(4,128)(2,1)S(1)}, u32[]{:S(2)}, u32[]{:S(2)}) async-start(bf16[4,4,16384]{2,1,0:T(4,128)(2,1)} %reshape.261), calls=%async_computation.1 | async-start | bytes 1048576 | tf_op jit(solution)/shard_map/all_to_all | solution.py:124
  105.9 406.3 %reduce-scatter.3.cloned.1.call-start = ((), (), s32[]{:S(2)}) async-start(), calls=%async_computation.5 | async-start | bytes 20971520 | tf_op jit(solution)/shard_map/reduce_scatter | solution.py:185
  155.0 9.2 copy-start.1
  231.4 436.7 %all-gather.2.cloned.1.call-start = ((), (), s32[]{:S(2)}) async-start(), calls=%async_computation.6 | async-start | bytes 10485760 | tf_op jit(solution)/shard_map/all_gather | solution.py:197
  231.5 11.4 %copy-start.5 = (f32[2]{0:T(128)S(1)}, f32[2]{0:T(128)}, u32[]{:S(2)}) copy-start(f32[2]{0:T(128)} %param.17) | copy-start | bytes 28
  517.8 207.6 %all-reduce.7.cloned.1.call-start = ((), (), s32[]{:S(2)}) async-start(), calls=%async_computation.7 | async-start | bytes 1048576 | tf_op jit(solution)/shard_map/psum | solution.py:164
  676.7 55.2 %copy-start.2 = (f32[16,128,128]{2,1,0:T(8,128)S(1)}, f32[16,128,128]{2,1,0:T(8,128)}, u32[]{:S(2)}) copy-start(f32[16,128,128]{2,1,0:T(8,128)} %copy.119) | copy-start | bytes 3145732
  693.6 403.3 %reduce-scatter.5.cloned.1.call-start = ((), (), s32[]{:S(2)}) async-start(), calls=%async_computation.8 | async-start | bytes 20971520 | tf_op jit(solution)/shard_map/reduce_scatter | solution.py:185
  1096.9 11.5 %copy-start = (f32[64,64,256]{2,0,1:T(8,128)S(1)}, f32[64,64,256]{2,0,1:T(8,128)}, u32[]{:S(2)}) copy-start(f32[64,64,256]{2,0,1:T(8,128)} %reduce-scatter.5.cloned.1.call-done) | copy-start | bytes 12582916
Sparse Core Ops, SparseCore 0:
  89.5 36.1 all-reduce.4
  231.6 280.5 reduce-scatter.2
  517.9 150.2 all-gather.1
  693.8 31.5 all-reduce.6
  816.1 280.7 reduce-scatter.4
where the time goes:
time: 1130 us; the launch traced here: 1120 us
  waiting for transfers between devices  754 us (67%)
  matrix products  169 us (15%)
  local copies, waits for them, and re-layouts  82.4 us (7%)
  other arithmetic  45.1 us (4%)
  blocking collectives  33.2 us (3%)
  between operations  14.5 us (1%)
    reduce_scatter x2, waiting for transfers between devices, spread(): lax.psum_scatter(result.reshape(row_share * lax.axis_size('bin'), slab_de...  550 us
    all_gather x1, waiting for transfers between devices, on_device(): lax.all_gather(first.astype(jnp.bfloat16), 'bin', axis=0, tiled=True)  150 us
    psum x2, waiting for transfers between devices, back_project(): projection = lax.psum(partial_value, 'slab')  50.4 us
    reshape x2, local copies, waits for them, and re-layouts, spread(): result.reshape(row_share * lax.axis_size('bin'), slab_depth, map_side)  39.1 us
    dot_general x2, matrix products, back_project(): jnp.einsum('pjk,ki->pij', slices, flat_folded, preferred_element_type=jnp...  34.6 us
    psum x2, blocking collectives, back_project(): sheets = lax.psum(sheets, 'slab').astype(jnp.bfloat16)  33.2 us
    dynamic_update_slice x8, other arithmetic, on_device(): slices = lax.map(make_slice, angles)  30.2 us
    dot_general x2, matrix products, back_project(): jnp.einsum('pjk,pij->ki', slices, sheets, preferred_element_type=jnp.floa...  29.6 us
  transfers between devices with their start and end apart: 7, of which 6 were waited for; matrix products, arithmetic and copies ran while one was open for 2% of the time, Pallas kernels for 0%

commit v1 on v0

v1 whole, which is shorter than its diff:
```python
import functools
import math

import jax
import jax.numpy as jnp
import numpy as np
from jax import lax
from jax.experimental import pallas as pl
from jax.experimental.pallas import tpu as pltpu
from jax.sharding import PartitionSpec as P

AMP_CONTRAST = 0.1
PHASE_RATE = 60.0
BLOCK = 16
WINDOW = 24
SMEM = pltpu.SMEM


def vmem():
    return pl.BlockSpec(memory_space=pltpu.VMEM)


def smem():
    return pl.BlockSpec(memory_space=SMEM)


def pool_table(image_side, map_side):
    row_index = np.arange(image_side)[:, None]
    col_index = np.arange(map_side)[None, :]
    return 0.5 * np.maximum(0.0, 1.0 - np.abs(col_index - 2.0 * row_index - 0.5) / 2.0)


def hartley_table(image_side):
    index_row = np.arange(image_side)
    phase_index = index_row[:, None] * index_row[None, :] % image_side
    angle_table = 2.0 * math.pi / image_side * phase_index
    table = (np.cos(angle_table) + np.sin(angle_table)) / math.sqrt(image_side)
    high = table.astype(jnp.bfloat16)
    low = (table - high.astype(np.float64)).astype(jnp.bfloat16)
    return jnp.asarray(np.concatenate([high, low], axis=1))


def ctf_table(defocus, image_side):
    index_row = jnp.arange(image_side, dtype=jnp.int32)
    frequency = (
        jnp.where(index_row < image_side // 2, index_row, index_row - image_side).astype(
            jnp.float32
        )
        / image_side
    )
    part = PHASE_RATE * defocus[:, None] * (frequency * frequency)[None, :]
    shifted = part + math.asin(AMP_CONTRAST)
    return -(
        jnp.sin(shifted)[:, :, None] * jnp.cos(part)[:, None, :]
        + jnp.cos(shifted)[:, :, None] * jnp.sin(part)[:, None, :]
    )


def geometry(angles, first_row, row_blocks, first_plane, plane_blocks, image_side, map_side):
    middle = map_side / 2.0
    scale = 0.25 / math.sqrt(map_side)
    cosine, sine = jnp.cos(angles), jnp.sin(angles)
    y_low = (first_row + BLOCK * jnp.arange(row_blocks)).astype(jnp.float32) + 0.5 - middle
    z_low = (first_plane + BLOCK * jnp.arange(plane_blocks)).astype(jnp.float32) + 0.5 - middle
    y_part = y_low[:, None] * cosine[None, :]
    z_part = z_low[:, None] * sine[None, :]
    y_edge = y_part + jnp.minimum(0.0, (BLOCK - 1) * cosine)[None, :]
    z_edge = z_part + jnp.minimum(0.0, (BLOCK - 1) * sine)[None, :]
    least = y_edge[:, None, :] + z_edge[None, :, :]
    column = jnp.floor((least - 3.0 + middle) / 16.0).astype(jnp.int32) * 8
    start = jnp.clip(column, 0, image_side - WINDOW)
    offset = scale * (
        y_part[:, None, :] + z_part[None, :, :] - (2.0 * start.astype(jnp.float32) + 1.0 - middle)
    )
    direction = jnp.stack([cosine, sine]) * scale
    return direction.reshape(-1), start.reshape(-1), offset.reshape(-1)


def local_tables(map_side):
    lane = lax.broadcasted_iota(jnp.int32, (8, BLOCK * BLOCK), 1)
    row = lax.broadcasted_iota(jnp.int32, (8, BLOCK * BLOCK), 0).astype(jnp.float32)
    y_local = (lane // BLOCK).astype(jnp.float32)
    z_local = (lane % BLOCK).astype(jnp.float32)
    scale = 0.25 / math.sqrt(map_side)
    rows = [(2.0 * scale) * (row + 8.0 * k) for k in range(WINDOW // 8)]
    return y_local, z_local, rows


def make_window(tables, direction, offset, pose, base, poses, map_side):
    y_local, z_local, rows = tables
    peak = 0.5 / math.sqrt(map_side)
    line = y_local * direction[pose] + z_local * direction[poses + pose] + offset[base + pose]
    return [jnp.maximum(0.0, peak - jnp.abs(line - r)) for r in rows]


def fill_windows(w_ref, tables, direction, offset, block, poses, map_side):
    base = block * poses

    def pair(k, _):
        parts = []
        for half in range(2):
            parts += make_window(
                tables, direction, offset, 2 * k + half, base, poses, map_side
            )
        at = pl.multiple_of(k * 2 * WINDOW, 2 * WINDOW)
        w_ref[pl.ds(at, 2 * WINDOW), :] = jnp.concatenate(parts, axis=0).astype(jnp.bfloat16)
        return 0

    lax.fori_loop(0, poses // 2, pair, 0, unroll=min(8, poses // 2))


def add_projection(outs, prod_ref, start, block, poses):
    base = block * poses
    share = poses // len(outs)

    for part, out in enumerate(outs):

        def one(k, _, part=part, out=out):
            pose = part * share + k
            at = pl.multiple_of(start[base + pose], 8)
            rows = pl.multiple_of(pose * WINDOW, 8)
            out[k, pl.ds(at, WINDOW), :] += prod_ref[pl.ds(rows, WINDOW), :]
            return 0

        lax.fori_loop(0, share, one, 0, unroll=min(8, share))


def first_projection_kernel(
    map_side, poses, plane_blocks, row_blocks, direction, start, offset, dens, pool_t, keep, send,
    w_ref, prod_ref
):
    step = pl.program_id(0)

    @pl.when(step == 0)
    def _():
        keep[...] = jnp.zeros_like(keep)
        send[...] = jnp.zeros_like(send)

    tables = local_tables(map_side)

    def block(k, _):
        row, plane = k // plane_blocks, k % plane_blocks
        rows = pl.ds(pl.multiple_of(row * BLOCK, BLOCK), BLOCK)
        planes = pl.ds(pl.multiple_of(plane * BLOCK, BLOCK), BLOCK)
        values = dens[rows, planes, :].reshape(BLOCK * BLOCK, map_side)
        folded = jnp.dot(values, pool_t[...], preferred_element_type=jnp.float32)
        index = step * row_blocks * plane_blocks + k
        fill_windows(w_ref, tables, direction, offset, index, poses, map_side)
        prod_ref[...] = jnp.dot(
            w_ref[...], folded.astype(jnp.bfloat16), preferred_element_type=jnp.float32
        )
        add_projection((keep, send), prod_ref, start, index, poses)
        return 0

    lax.fori_loop(0, row_blocks * plane_blocks, block, 0)


def first_projection(density, pool_t, geo, poses):
    map_side, depth, _ = density.shape
    side = pool_t.shape[1]
    row_blocks = 2
    half = jax.ShapeDtypeStruct((poses // 2, side, side), jnp.float32)
    return pl.pallas_call(
        functools.partial(first_projection_kernel, map_side, poses, depth // BLOCK, row_blocks),
        grid=(map_side // (BLOCK * row_blocks),),
        in_specs=[smem(), smem(), smem(),
                  pl.BlockSpec((BLOCK * row_blocks, depth, map_side), lambda i: (i, 0, 0)),
                  vmem()],
        out_specs=[vmem(), vmem()],
        out_shape=[half, half],
        scratch_shapes=[
            pltpu.VMEM((poses * WINDOW, BLOCK * BLOCK), jnp.bfloat16),
            pltpu.VMEM((poses * WINDOW, side), jnp.float32),
        ],
        name="first_projection",
    )(*geo, density, pool_t)


def pick_kernel(count, order, images, *rest):
    outs, sems = rest[:-1], rest[-1]
    each = count // len(outs)
    copies = [
        pltpu.make_async_copy(images.at[order[k]], outs[k // each].at[k % each], sems.at[k])
        for k in range(count)
    ]
    for copy in copies:
        copy.start()
    for copy in copies:
        copy.wait()


def pick_images(images, order, groups):
    count = order.shape[0]
    _, side, _ = images.shape
    out = jax.ShapeDtypeStruct((count // groups, side, side), images.dtype)
    return pl.pallas_call(
        functools.partial(pick_kernel, count),
        in_specs=[smem(), pl.BlockSpec(memory_space=pl.ANY)],
        out_specs=[pl.BlockSpec(memory_space=pl.ANY)] * groups,
        out_shape=[out] * groups,
        scratch_shapes=[pltpu.SemaphoreType.DMA((count,))],
        name="pick_images",
    )(order, images)


def times_hartley(value, table):
    count, side = value.shape
    high = value.astype(jnp.bfloat16)
    low = (value - high.astype(jnp.float32)).astype(jnp.bfloat16)
    both = jnp.dot(high, table, preferred_element_type=jnp.float32)
    rest = jnp.dot(low, table[:, :side], preferred_element_type=jnp.float32)
    return both[:, :side] + (both[:, side:] + rest)


def spectrum_kernel(groups, each, classes, label, ctf, table, *refs):
    images, (keep, send) = refs[:groups], refs[groups:]
    half = keep.shape[0]
    side = keep.shape[1]
    keep[...] = jnp.zeros_like(keep)
    send[...] = jnp.zeros_like(send)
    hart = table[...]
    for group in range(groups):
        pixels = images[group][...].reshape(each * side, side)
        both = jnp.dot(pixels, hart, preferred_element_type=jnp.float32)
        along = (both[:, :side] + both[:, side:]).reshape(each, side, side)
        turned = jnp.concatenate([along[k].T for k in range(each)], axis=0)
        full = times_hartley(turned, hart).reshape(each, side, side)
        for k in range(each):
            mark = label[group * each + k]
            pose = mark // classes
            value = ctf[mark % classes] * full[k]

            @pl.when(jnp.logical_and(mark >= 0, pose < half))
            def _(pose=pose, value=value):
                keep[pose] += value

            @pl.when(pose >= half)
            def _(pose=pose, value=value):
                send[pose - half] += value

    for out in (keep, send):
        for pose in range(half):
            out[pose] = out[pose].T


def image_sums(images, label, ctf, table, poses):
    each, side, _ = images[0].shape
    half = jax.ShapeDtypeStruct((poses // 2, side, side), jnp.float32)
    return pl.pallas_call(
        functools.partial(spectrum_kernel, len(images), each, ctf.shape[0]),
        in_specs=[smem(), vmem(), vmem()] + [vmem()] * len(images),
        out_specs=[vmem(), vmem()],
        out_shape=[half, half],
        name="image_sums",
    )(label, ctf, table, *images)


def filter_kernel(weight, tally, ctf, table, power, *refs):
    proj, total, out = refs[:-2], refs[-2], refs[-1]
    owned, side, _ = out.shape
    classes = ctf.shape[0]
    hart = table[...]
    value = proj[0][...]
    for part in proj[1:]:
        value = value + part[...]
    along = times_hartley(value.reshape(owned * side, side), hart)
    turned = jnp.concatenate([along[k * side : (k + 1) * side].T for k in range(owned)], axis=0)
    full = times_hartley(turned, hart)
    parts = []
    for k in range(owned):
        gain = jnp.zeros((side, side), jnp.float32)
        for c in range(classes):
            gain = gain + tally[k * classes + c] * (ctf[c] * ctf[c])
        parts.append(weight * (gain * full[k * side : (k + 1) * side] - total[k]))
    along = times_hartley(jnp.concatenate(parts, axis=0), hart)
    turned = jnp.concatenate([along[k * side : (k + 1) * side].T for k in range(owned)], axis=0)
    field = times_hartley(turned, hart)
    out[...] = field.reshape(owned, side, side).astype(out.dtype)


def residual_field(parts, total, tally, ctf, table, weight):
    owned, side, _ = total.shape

    def kernel(tally, ctf, table, *refs):
        filter_kernel(weight, tally, ctf, table, None, *refs)

    return pl.pallas_call(
        kernel,
        in_specs=[smem(), vmem(), vmem()] + [vmem()] * (len(parts) + 1),
        out_specs=vmem(),
        out_shape=jax.ShapeDtypeStruct((owned, side, side), jnp.bfloat16),
        name="residual_field",
    )(tally, ctf, table, *parts, total)


def load_fields(field, fields):
    at = 0
    for part in fields:
        count = part.shape[0]
        field[at : at + count] = part[...].astype(jnp.float32)
        at += count


def gather_windows(f_ref, field, start, block, poses):
    base = block * poses

    def pair(k, _):
        parts = []
        for half in range(2):
            at = pl.multiple_of(start[base + 2 * k + half], 8)
            parts.append(field[2 * k + half, pl.ds(at, WINDOW), :])
        rows = pl.multiple_of(k * 2 * WINDOW, 2 * WINDOW)
        f_ref[pl.ds(rows, 2 * WINDOW), :] = jnp.concatenate(parts, axis=0).astype(jnp.bfloat16)
        return 0

    lax.fori_loop(0, poses // 2, pair, 0, unroll=min(8, poses // 2))


def block_gradient(w_ref, f_ref, pool2):
    back = lax.dot_general(
        w_ref[...], f_ref[...], (((0,), (0,)), ((), ())), preferred_element_type=jnp.float32
    )
    high = back.astype(jnp.bfloat16)
    low = (back - high.astype(jnp.float32)).astype(jnp.bfloat16)
    return jnp.dot(
        jnp.concatenate([high, low], axis=1), pool2[...], preferred_element_type=jnp.float32
    )


def step_kernel(
    map_side, poses, plane_blocks, parts, bin_ref, direction, start, offset, sizes, dens, pool2,
    pool_t, *refs
):
    fields = refs[:parts]
    first, keep, send, field, w_ref, f_ref, prod_ref = refs[parts:]
    step = pl.program_id(0)

    @pl.when(step == 0)
    def _():
        keep[...] = jnp.zeros_like(keep)
        send[...] = jnp.zeros_like(send)
        load_fields(field, fields)

    tables = local_tables(map_side)

    def block(k, _):
        planes = pl.ds(pl.multiple_of(k * BLOCK, BLOCK), BLOCK)
        index = step * plane_blocks + k
        fill_windows(w_ref, tables, direction, offset, index, poses, map_side)
        gather_windows(f_ref, field, start, index, poses)
        grad = block_gradient(w_ref, f_ref, pool2)
        values = dens[:, planes, :].reshape(BLOCK * BLOCK, map_side).astype(jnp.float32)
        moved = values - sizes[0] * grad
        first[:, planes, :] = moved.reshape(BLOCK, BLOCK, map_side)
        folded = jnp.dot(
            moved.astype(jnp.bfloat16), pool_t[...], preferred_element_type=jnp.float32
        )
        prod_ref[...] = jnp.dot(
            w_ref[...], folded.astype(jnp.bfloat16), preferred_element_type=jnp.float32
        )
        add_projection((keep, send), prod_ref, start, index, poses)
        return 0

    lax.fori_loop(0, plane_blocks, block, 0)


def take_step(density, fields, geo, sizes, bin_index, pool2, pool_t, poses, row_share):
    map_side, depth, _ = density.shape
    side = pool_t.shape[1]
    half = jax.ShapeDtypeStruct((poses // 2, side, side), jnp.float32)
    row_blocks = row_share // BLOCK
    rows = (BLOCK, depth, map_side)
    scalars = (geo[0], geo[1], geo[2], sizes)
    return pl.pallas_call(
        functools.partial(step_kernel, map_side, poses, depth // BLOCK, len(fields)),
        grid_spec=pltpu.PrefetchScalarGridSpec(
            num_scalar_prefetch=1,
            grid=(row_blocks,),
            in_specs=[smem()] * len(scalars)
            + [pl.BlockSpec(rows, lambda i, at: (at[0] * row_blocks + i, 0, 0))]
            + [vmem()] * (2 + len(fields)),
            out_specs=[pl.BlockSpec(rows, lambda i, at: (i, 0, 0)), vmem(), vmem()],
            scratch_shapes=[
                pltpu.VMEM((poses, side, side), jnp.float32),
                pltpu.VMEM((poses * WINDOW, BLOCK * BLOCK), jnp.bfloat16),
                pltpu.VMEM((poses * WINDOW, side), jnp.bfloat16),
                pltpu.VMEM((poses * WINDOW, side), jnp.float32),
            ],
        ),
        out_shape=[jax.ShapeDtypeStruct((row_share, depth, map_side), jnp.float32), half, half],
        name="take_step",
    )(bin_index.reshape(1), *scalars, density, pool2, pool_t, *fields)


def finish_kernel(
    map_side, poses, plane_blocks, parts, direction, start, offset, sizes, first, pool2, *refs
):
    fields = refs[:parts]
    gradient, refined, field, w_ref, f_ref = refs[parts:]
    step = pl.program_id(0)

    @pl.when(step == 0)
    def _():
        load_fields(field, fields)

    tables = local_tables(map_side)

    def block(k, _):
        planes = pl.ds(pl.multiple_of(k * BLOCK, BLOCK), BLOCK)
        index = step * plane_blocks + k
        fill_windows(w_ref, tables, direction, offset, index, poses, map_side)
        gather_windows(f_ref, field, start, index, poses)
        grad = block_gradient(w_ref, f_ref, pool2).reshape(BLOCK, BLOCK, map_side)
        gradient[:, planes, :] = grad
        refined[:, planes, :] = first[:, planes, :] - sizes[1] * grad
        return 0

    lax.fori_loop(0, plane_blocks, block, 0)


def finish(first, fields, geo, sizes, pool2, poses):
    row_share, depth, map_side = first.shape
    side = pool2.shape[0] // 2
    rows = pl.BlockSpec((BLOCK, depth, map_side), lambda i: (i, 0, 0))
    out = jax.ShapeDtypeStruct(first.shape, jnp.float32)
    return pl.pallas_call(
        functools.partial(finish_kernel, map_side, poses, depth // BLOCK, len(fields)),
        grid=(row_share // BLOCK,),
        in_specs=[smem()] * 4 + [rows] + [vmem()] * (1 + len(fields)),
        out_specs=[rows, rows],
        out_shape=[out, out],
        scratch_shapes=[
            pltpu.VMEM((poses, side, side), jnp.float32),
            pltpu.VMEM((poses * WINDOW, BLOCK * BLOCK), jnp.bfloat16),
            pltpu.VMEM((poses * WINDOW, side), jnp.bfloat16),
        ],
        name="finish",
    )(*geo, sizes, first, pool2, *fields)


def on_device(
    density, images, image_bin, image_pose, image_class, defocus, pose_offset, step_sizes
):
    bins = lax.axis_size("bin")
    slabs = lax.axis_size("slab")
    chips = slabs // 2
    bin_index = lax.axis_index("bin")
    slab_index = lax.axis_index("slab")
    chip, core = slab_index // 2, slab_index % 2
    map_side, depth, _ = density.shape
    image_count, side, _ = images.shape
    pose_count = pose_offset.shape[1]
    classes = defocus.shape[0]
    capacity = image_count // 4
    row_share = map_side // bins
    owned = pose_count // slabs
    weight = 16.0 * pose_count / (image_count * slabs)

    def to_core(value):
        return lax.ppermute(value, "slab", [(s, s ^ 1) for s in range(slabs)])

    def to_chip(value, shift):
        return lax.ppermute(
            value, "slab", [(s, (s + 2 * shift) % slabs) for s in range(slabs)]
        )

    def to_bin(value, shift):
        return lax.ppermute(value, "bin", [(b, (b + shift) % bins) for b in range(bins)])

    cores_on, chips_on, place = jnp.meshgrid(
        jnp.arange(2), jnp.arange(chips), jnp.arange(owned), indexing="ij"
    )
    owner = (chip + chips_on) % chips * 2 + (core + cores_on) % 2
    own_order = (owner * owned + place).reshape(-1)
    own_offset = jnp.take(
        lax.dynamic_index_in_dim(pose_offset, bin_index, 0, keepdims=False), own_order
    )
    own_angles = math.pi * (bin_index.astype(jnp.float32) + own_offset) / bins
    bin_order = (bin_index + jnp.arange(bins)) % bins
    rel = jnp.take(jnp.take(pose_offset, bin_order, axis=0), own_order, axis=1)
    rel = math.pi * (bin_order.astype(jnp.float32)[:, None] + rel) / bins
    rel = rel.reshape(bins, 2, chips, owned).transpose(1, 2, 0, 3).reshape(-1)
    poses = bins * pose_count
    first_plane = slab_index * depth
    own_geo = geometry(
        own_angles, 0, map_side // BLOCK, first_plane, depth // BLOCK, side, map_side
    )
    geo = geometry(
        rel, bin_index * row_share, row_share // BLOCK, first_plane, depth // BLOCK, side, map_side
    )
    pooling = pool_table(side, map_side).astype(jnp.bfloat16)
    pool_t = jnp.asarray(pooling.T)
    pool2 = jnp.asarray(np.concatenate([pooling, pooling], axis=0))
    table = hartley_table(side)
    ctf = ctf_table(defocus, side)

    target = image_bin[:, 0]
    chosen = (target[:, None] == jnp.arange(bins, dtype=jnp.int32)[None, :]).astype(jnp.int32)
    rank = jnp.sum((jnp.cumsum(chosen, axis=0) - chosen) * chosen, axis=1)
    slot = (target - bin_index) % bins * capacity + rank
    placement = jnp.arange(bins * capacity, dtype=jnp.int32)[:, None] == slot[None, :]
    order = jnp.sum(
        jnp.where(placement, jnp.arange(image_count, dtype=jnp.int32)[None, :], 0), axis=1
    )
    mark = image_pose * classes + image_class + 1
    marks = jnp.sum(jnp.where(placement, mark[None, :], 0), axis=1) - 1
    picked = pick_images(images, order, bins)
    marks = marks.reshape(bins, capacity)
    got_images = [picked[0]] + [to_bin(picked[d], d) for d in range(1, bins)]
    got_marks = [marks[0]] + [to_bin(marks[d], d) for d in range(1, bins)]
    got_marks = jnp.concatenate(got_marks)
    got_pose, got_class = got_marks // classes, got_marks % classes
    at = jnp.argmax(
        (got_pose[:, None] == own_order[None, :]).astype(jnp.int32), axis=1
    ).astype(jnp.int32)
    label = jnp.where(got_marks >= 0, at * classes + got_class, -1)
    tally = jnp.sum(
        (
            label[:, None]
            == jnp.arange(pose_count * classes, dtype=jnp.int32)[None, :]
        ).astype(jnp.float32),
        axis=0,
    ).reshape(2, chips, owned * classes)

    def reduce_slab(keep, send):
        got = to_core(send)
        sums = [keep[d] + got[d] for d in range(chips)]
        moved = [to_chip(sums[d], d) for d in range(1, chips)]
        return [sums[0]] + moved

    tally = functools.reduce(jnp.add, reduce_slab(tally[0], tally[1]))

    def split(value):
        return value.reshape(chips, -1, *value.shape[1:])

    keep, send = first_projection(density, pool_t, own_geo, pose_count)
    proj_parts = reduce_slab(split(keep), split(send))
    keep, send = image_sums(got_images, label, ctf, table, pose_count)
    total = functools.reduce(jnp.add, reduce_slab(split(keep), split(send)))

    def share_field(field):
        near = [field] + [to_bin(field, bins - d) for d in range(1, bins)]
        near = jnp.concatenate(near, axis=0)
        row = [near] + [to_chip(near, chips - d) for d in range(1, chips)]
        return row + [to_core(part) for part in row]

    field = residual_field(proj_parts, total, tally, ctf, table, weight)
    first, keep, send = take_step(
        density, share_field(field), geo, step_sizes, bin_index, pool2, pool_t, poses, row_share
    )
    parts = functools.reduce(jnp.add, reduce_slab(split(keep), split(send)))
    parts = parts.reshape(bins, owned, side, side)
    parts = [parts[0]] + [to_bin(parts[d], d) for d in range(1, bins)]
    field = residual_field(parts, total, tally, ctf, table, weight)
    gradient, refined = finish(first, share_field(field), geo, step_sizes, pool2, poses)
    return (gradient, refined)


def solution(mesh):
    return jax.shard_map(
        on_device,
        mesh=mesh,
        in_specs=(
            P("grp", "slab", None),
            P(("grp", "bin", "slab"), None, None),
            P(("grp", "bin", "slab"), None),
            P(("grp", "bin", "slab")),
            P(("grp", "bin", "slab")),
            P("grp"),
            P("grp", None),
            P(),
        ),
        out_specs=(P(("grp", "bin"), "slab", None), P(("grp", "bin"), "slab", None)),
        check_vma=False,
    )
```

time: 1130 us -> 208 us (0.18)
  waiting for transfers between devices: 754 us -> 54.4 us
  matrix products: 169 us -> 0 us
  Pallas kernels: 0 us -> 92.4 us
  local copies, waits for them, and re-layouts: 82.4 us -> 9.67 us
  blocking collectives: 33.2 us -> 0 us
  other arithmetic: 45.1 us -> 16.5 us
  starting transfers between devices: 10.9 us -> 33.2 us
  between operations: 14.5 us -> 0.97 us
    reduce_scatter x2 -> x0, waiting for transfers between devices: 550 us -> none  [spread(): lax.psum_scatter(result.reshape(row_share * lax.axis_size('bin'), slab_de...]
    dot_general x48 -> x0, matrix products: 169 us -> none  [the longest x2 34.6 us: back_project(): jnp.einsum('pjk,ki->pij', slices, flat_folded, preferred_element_type=jnp...]
    all_gather x1 -> x0, waiting for transfers between devices: 150 us -> none  [on_device(): lax.all_gather(first.astype(jnp.bfloat16), 'bin', axis=0, tiled=True)]
    pallas_call x0 -> x7, Pallas kernels: none -> 92.4 us  [the longest x1 26 us: first_projection(): pl.pallas_call(functools.partial(first_projection_kernel, map_side, poses...]
    ppermute x0 -> x29, waiting for transfers between devices: none -> 54.4 us  [the longest x6 25.2 us: to_chip(): lax.ppermute(value, 'slab', [(s, (s + 2 * shift) % slabs) for s in range(...]
    psum x2 -> x0, waiting for transfers between devices: 50.4 us -> none  [back_project(): projection = lax.psum(partial_value, 'slab')]
    reshape x7 -> x0, local copies, waits for them, and re-layouts: 41.4 us -> none  [the longest x2 39.1 us: spread(): result.reshape(row_share * lax.axis_size('bin'), slab_depth, map_side)]
    psum x2 -> x0, blocking collectives: 33.2 us -> none  [back_project(): sheets = lax.psum(sheets, 'slab').astype(jnp.bfloat16)]
  transfers between devices with their start and end apart: 7 -> 29, of which waited for: 6 -> 18; matrix products, arithmetic and copies ran while one was open for 2% -> 7% of each run, Pallas kernels for 0% -> 23%
where the time goes in v1:
time: 208 us; the launch traced here: 207 us
  Pallas kernels  92.4 us (44%)
  waiting for transfers between devices  54.4 us (26%)
  starting transfers between devices  33.2 us (16%)
  other arithmetic  16.5 us (8%)
  local copies, waits for them, and re-layouts  9.67 us (5%)
    pallas_call x1, Pallas kernels, first_projection(): pl.pallas_call(functools.partial(first_projection_kernel, map_side, poses...  26 us
    ppermute x6, waiting for transfers between devices, to_chip(): lax.ppermute(value, 'slab', [(s, (s + 2 * shift) % slabs) for s in range(...  25.2 us
    ppermute x15, starting transfers between devices, to_bin(): lax.ppermute(value, 'bin', [(b, (b + shift) % bins) for b in range(bins)])  23.9 us
    pallas_call x1, Pallas kernels, take_step(): pl.pallas_call(functools.partial(step_kernel, map_side, poses, depth // B...  23.8 us
    ppermute x15, waiting for transfers between devices, to_bin(): lax.ppermute(value, 'bin', [(b, (b + shift) % bins) for b in range(bins)])  22.6 us
    pallas_call x1, Pallas kernels, pick_images(): pl.pallas_call(functools.partial(pick_kernel, count), in_specs=[smem(), p...  17.8 us
    pallas_call x1, Pallas kernels, finish(): pl.pallas_call(functools.partial(finish_kernel, map_side, poses, depth //...  14.5 us
    ppermute x6, starting transfers between devices, to_chip(): lax.ppermute(value, 'slab', [(s, (s + 2 * shift) % slabs) for s in range(...  8.66 us
  transfers between devices with their start and end apart: 29, of which 18 were waited for; matrix products, arithmetic and copies ran while one was open for 7% of the time, Pallas kernels for 23%

profile of v1, /device:TPU:0, one launch (start us, length us, event | category | flops | bytes accessed | tf_op | source)
XLA Modules:
  0.0 207.2 jit_solution(2762155090521219806)
XLA Ops:
  0.7 0.7 fusion.10
  1.4 0.8 select_reduce_fusion.2
  2.3 0.7 fusion.19
  3.0 0.7 select_reduce_fusion
  3.7 5.1 %collective-permute-start.2 = (s32[4]{0:T(128)S(1)}, s32[4]{0:T(128)S(1)}, u32[]{:S(2)}, u32[]{:S(2)}) collective-permute-start(s32[4]{0:T(128)S(1)} %get-tuple-element.56), channel_id=1, source_target_pairs={{0,12},{4,0},{8,4},{12,8},{1,13},{5,1},{9,5},{13,9},{2,14},{6,2},{... | collective-permute-start | bytes 56 | tf_op jit(solution)/shard_map/ppermute | solution.py:468
  8.8 1.0 collective-permute-start
  10.8 0.6 gather_fusion.2
  11.7 0.6 mul.402.direction
  12.9 0.6 subtract_multiply_fusion.offset
  13.5 26.0 %first_projection.1 = (f32[4,128,128]{2,1,0:T(8,128)}, f32[4,128,128]{2,1,0:T(8,128)}) custom-call(f32[16]{0:T(128)} %mul.402.direction, s32[512]{0:T(512)} %copy-done.17, f32[512]{0:T(512)} %subtract_multiply_fusion.offset, bf16[256,64,256]{2,1,0:T(8,128)(2,1)} %dens.3, bf16[256,128]{1,0:T(8,128)(2,1)} %constant.237.clone.pool_t), custom_call_target="tpu_custom_call" | custom-call | tf_op jit(solution)/shard_map/first_projection/pallas_call | solution.py:163
  39.6 17.8 %pick_images.1 = (bf16[4,128,128]{2,1,0:T(8,128)(2,1)}, bf16[4,128,128]{2,1,0:T(8,128)(2,1)}, bf16[4,128,128]{2,1,0:T(8,128)(2,1)}, bf16[4,128,128]{2,1,0:T(8,128)(2,1)}) custom-call(s32[16]{0:T(128)} %get-tuple-element.26.order, bf16[16,128,128]{2,1,0:T(8,128)(2,1)} %images.1), custom_call_target="tpu_custom_call" | custom-call | tf_op jit(solution)/shard_map/pick_images/pallas_call | solution.py:196
  57.4 2.5 %collective-permute-start.7 = (bf16[4,128,128]{2,1,0:T(8,128)(2,1)}, bf16[4,128,128]{2,1,0:T(8,128)(2,1)S(1)}, u32[]{:S(2)}, u32[]{:S(2)}) collective-permute-start(bf16[4,128,128]{2,1,0:T(8,128)(2,1)} %get-tuple-element.18), channel_id=1, source_target_pairs={{0,4},{4,8},{8,12},{12,0},{1,5},{5,9},{9,13},{13,1},{2,6},{6,10},{... | collective-permute-start | bytes 393224 | tf_op jit(solution)/shard_map/ppermute | solution.py:468
  62.2 1.6 add_negate_fusion.ctf
  63.8 0.9 collective-permute-start.8
  64.7 1.5 collective-permute-start.9
  66.2 0.7 iota_reduce_fusion
  67.2 1.2 collective-permute-done.3
  68.4 1.5 collective-permute-start.4
  69.9 3.2 %collective-permute-done.8.refs_2_ = bf16[4,128,128]{2,1,0:T(8,128)(2,1)S(1)} collective-permute-done((bf16[4,128,128]{2,1,0:T(8,128)(2,1)}, bf16[4,128,128]{2,1,0:T(8,128)(2,1)S(1)}, u32[]{:S(2)}, u32[]{:S(2)}) %collective-permute-start.8) | collective-permute-done | bytes 131104 | tf_op jit(solution)/shard_map/ppermute | solution.py:468
  73.1 0.6 copy-done.10
  73.8 4.5 %image_sums.1 = (f32[4,128,128]{2,1,0:T(8,128)}, f32[4,128,128]{2,1,0:T(8,128)}) custom-call(s32[16]{0:T(128)} %copy-done.18, f32[16,128,128]{2,1,0:T(8,128)} %add_negate_fusion.ctf, bf16[128,256]{1,0:T(8,128)(2,1)} %constant.239.clone.table, bf16[4,128,128]{2,1,0:T(8,128)(2,1)} %get-tuple-element.17.refs_0_, bf16[4,128,128]{2,1,0:T(8,128)(2,1)} %copy-done.9, ...), custom_call_target="tpu_custom_call" | custom-call | tf_op jit(solution)/shard_map/image_sums/pallas_call | solution.py:249
  78.8 1.2 collective-permute-done.10
  80.1 0.9 fusion.3
  81.0 1.6 collective-permute-start.11
  82.5 1.7 fusion.6
  84.7 1.8 collective-permute-done.11
  86.6 1.6 fusion.5.refs_2_.refs_4_
  88.2 1.3 collective-permute-done.6.refs_1_
  89.5 0.7 copy-done.12
  90.1 2.8 %residual_field.2 = bf16[2,128,128]{2,1,0:T(8,128)(2,1)} custom-call(f32[32]{0:T(128)} %fusion.36.tally, f32[16,128,128]{2,1,0:T(8,128)} %add_negate_fusion.ctf, bf16[128,256]{1,0:T(8,128)(2,1)} %constant.239.clone.table, f32[2,128,128]{2,1,0:T(8,128)} %get-tuple-element.40.refs_0_, f32[2,128,128]{2,1,0:T(8,128)} %copy-done.12, ...), custom_call_target="tpu_custom_call" | custom-call | tf_op jit(solution)/shard_map/residual_field/pallas_call | solution.py:287
  93.0 3.3 %collective-permute-start.14 = (bf16[2,128,128]{2,1,0:T(8,128)(2,1)}, bf16[2,128,128]{2,1,0:T(8,128)(2,1)S(1)}, u32[]{:S(2)}, u32[]{:S(2)}) collective-permute-start(bf16[2,128,128]{2,1,0:T(8,128)(2,1)} %residual_field.2), channel_id=1, source_target_pairs={{0,4},{4,8},{8,12},{12,0},{1,5},{5,9},{9,13},{13,1},{2,6},{6,10},{... | collective-permute-start | bytes 196616 | tf_op jit(solution)/shard_map/ppermute | solution.py:468
  96.2 1.7 collective-permute-start.13
  97.9 0.7 collective-permute-start.12
  98.7 1.3 collective-permute-done.14
  99.9 2.7 %collective-permute-done.13 = bf16[2,128,128]{2,1,0:T(8,128)(2,1)S(1)} collective-permute-done((bf16[2,128,128]{2,1,0:T(8,128)(2,1)}, bf16[2,128,128]{2,1,0:T(8,128)(2,1)S(1)}, u32[]{:S(2)}, u32[]{:S(2)}) %collective-permute-start.13) | collective-permute-done | bytes 65568 | tf_op jit(solution)/shard_map/ppermute | solution.py:468
  102.9 0.9 pad_maximum_fusion.refs_0_
  103.8 1.5 collective-permute-start.15
  105.5 5.0 %collective-permute-done.15.refs_1_ = bf16[8,128,128]{2,1,0:T(8,128)(2,1)S(1)} collective-permute-done((bf16[8,128,128]{2,1,0:T(8,128)(2,1)S(1)}, bf16[8,128,128]{2,1,0:T(8,128)(2,1)S(1)}, u32[]{:S(2)}, u32[]{:S(2)}) %collective-permute-start.15) | collective-permute-done | bytes 262176 | tf_op jit(solution)/shard_map/ppermute | solution.py:463
  110.6 0.7 mul.364.direction
  111.4 0.6 subtract_multiply_fusion.1.offset
  112.1 0.6 copy-done.4
  112.8 23.8 %take_step.1 = (f32[64,64,256]{2,1,0:T(8,128)}, f32[16,128,128]{2,1,0:T(8,128)}, f32[16,128,128]{2,1,0:T(8,128)}) custom-call(s32[1]{0:T(128)} %bitcast.6.bin_ref, f32[64]{0:T(128)} %mul.364.direction, s32[512]{0:T(512)} %copy-done.16, f32[512]{0:T(512)} %subtract_multiply_fusion.1.offset, f32[2]{0:T(128)} %sizes.3, bf16[256,64,256]{2,1,0:T(8,128)(2,1)} %dens.3, ...), custom_call_target="tpu_custom_call" | custom-call | tf_op jit(solution)/shard_map/take_step/pallas_call | solution.py:374
  137.2 2.5 %collective-permute-done.18 = f32[2,8,128,128]{3,2,1,0:T(8,128)S(1)} collective-permute-done((f32[2,8,128,128]{3,2,1,0:T(8,128)}, f32[2,8,128,128]{3,2,1,0:T(8,128)S(1)}, u32[]{:S(2)}, u32[]{:S(2)}) %collective-permute-start.18) | collective-permute-done | bytes 1048608 | tf_op jit(solution)/shard_map/ppermute | solution.py:460
  139.7 1.1 fusion
  140.8 1.8 collective-permute-start.19
  142.6 12.5 %collective-permute-done.19 = f32[8,128,128]{2,1,0:T(8,128)S(1)} collective-permute-done((f32[8,128,128]{2,1,0:T(8,128)S(1)}, f32[8,128,128]{2,1,0:T(8,128)S(1)}, u32[]{:S(2)}, u32[]{:S(2)}) %collective-permute-start.19) | collective-permute-done | bytes 524320 | tf_op jit(solution)/shard_map/ppermute | solution.py:463
  155.1 1.2 fusion.2
  156.3 0.7 fusion.42
  156.9 1.9 collective-permute-start.22
  158.8 1.6 collective-permute-start.21
  160.4 2.3 %collective-permute-done.22.refs_3_ = f32[2,128,128]{2,1,0:T(8,128)S(1)} collective-permute-done((f32[2,128,128]{2,1,0:T(8,128)S(1)}, f32[2,128,128]{2,1,0:T(8,128)S(1)}, u32[]{:S(2)}, u32[]{:S(2)}) %collective-permute-start.22) | collective-permute-done | bytes 131104 | tf_op jit(solution)/shard_map/ppermute | solution.py:468
  162.7 9.0 %collective-permute-done.21.refs_2_ = f32[2,128,128]{2,1,0:T(8,128)S(1)} collective-permute-done((f32[2,128,128]{2,1,0:T(8,128)S(1)}, f32[2,128,128]{2,1,0:T(8,128)S(1)}, u32[]{:S(2)}, u32[]{:S(2)}) %collective-permute-start.21) | collective-permute-done | bytes 131104 | tf_op jit(solution)/shard_map/ppermute | solution.py:468
  171.7 0.7 copy-done.14
  172.4 2.9 %residual_field.3 = bf16[2,128,128]{2,1,0:T(8,128)(2,1)} custom-call(f32[32]{0:T(128)} %fusion.36.tally, f32[16,128,128]{2,1,0:T(8,128)} %add_negate_fusion.ctf, bf16[128,256]{1,0:T(8,128)(2,1)} %constant.239.clone.table, f32[2,128,128]{2,1,0:T(8,128)} %get-tuple-element.38.refs_0_, f32[2,128,128]{2,1,0:T(8,128)} %copy-done.15, f32[2,128,128]{2,1,0:T(8,128)} %copy-done.14, ...), custom_call_target="tpu_custom_call" | custom-call | tf_op jit(solution)/shard_map/residual_field/pallas_call | solution.py:287
  175.4 0.8 collective-permute-start.24
  176.1 3.1 %collective-permute-start.23 = (bf16[2,128,128]{2,1,0:T(8,128)(2,1)}, bf16[2,128,128]{2,1,0:T(8,128)(2,1)S(1)}, u32[]{:S(2)}, u32[]{:S(2)}) collective-permute-start(bf16[2,128,128]{2,1,0:T(8,128)(2,1)} %residual_field.3), channel_id=1, source_target_pairs={{0,12},{4,0},{8,4},{12,8},{1,13},{5,1},{9,5},{13,9},{2,14},{6,2},{... | collective-permute-start | bytes 196616 | tf_op jit(solution)/shard_map/ppermute | solution.py:468
  179.2 2.6 %collective-permute-done.25 = bf16[2,128,128]{2,1,0:T(8,128)(2,1)S(1)} collective-permute-done((bf16[2,128,128]{2,1,0:T(8,128)(2,1)}, bf16[2,128,128]{2,1,0:T(8,128)(2,1)S(1)}, u32[]{:S(2)}, u32[]{:S(2)}) %collective-permute-start.25) | collective-permute-done | bytes 65568 | tf_op jit(solution)/shard_map/ppermute | solution.py:468
  181.8 1.2 collective-permute-done.24
  183.0 0.9 pad_maximum_fusion.1.refs_0_
  183.9 1.8 collective-permute-start.26
  185.7 4.6 %collective-permute-done.26.refs_1_ = bf16[8,128,128]{2,1,0:T(8,128)(2,1)S(1)} collective-permute-done((bf16[8,128,128]{2,1,0:T(8,128)(2,1)S(1)}, bf16[8,128,128]{2,1,0:T(8,128)(2,1)S(1)}, u32[]{:S(2)}, u32[]{:S(2)}) %collective-permute-start.26) | collective-permute-done | bytes 262176 | tf_op jit(solution)/shard_map/ppermute | solution.py:463
  190.4 1.5 collective-permute-done.28.refs_3_
  191.9 0.7 copy-done.8
  192.6 14.5 %finish.1 = (f32[64,64,256]{2,1,0:T(8,128)}, f32[64,64,256]{2,1,0:T(8,128)}) custom-call(f32[64]{0:T(128)} %mul.364.direction, s32[512]{0:T(512)} %copy-done.16, f32[512]{0:T(512)} %subtract_multiply_fusion.1.offset, f32[2]{0:T(128)} %sizes.3, f32[64,64,256]{2,1,0:T(8,128)} %get-tuple-element.23.first, bf16[256,256]{1,0:T(8,128)(2,1)} %constant.238.clone.pool2, ...), custom_call_target="tpu_custom_call" | custom-call | tf_op jit(solution)/shard_map/finish/pallas_call | solution.py:426
  (136 shorter events, 7.3 us)
Async XLA Ops:
  0.6 10.2 %copy-start = (f32[4,8]{1,0:T(4,128)S(1)}, f32[4,8]{1,0:T(4,128)}, u32[]{:S(2)}) copy-start(f32[4,8]{1,0:T(4,128)} %param.17) | copy-start | bytes 388
  3.7 60.0 %collective-permute-start.2 = (s32[4]{0:T(128)S(1)}, s32[4]{0:T(128)S(1)}, u32[]{:S(2)}, u32[]{:S(2)}) collective-permute-start(s32[4]{0:T(128)S(1)} %get-tuple-element.56), channel_id=1, source_target_pairs={{0,12},{4,0},{8,4},{12,8},{1,13},{5,1},{9,5},{13,9},{2,14},{6,2},{... | collective-permute-start | bytes 56 | tf_op jit(solution)/shard_map/ppermute | solution.py:468
  8.8 55.8 %collective-permute-start.1 = (s32[4]{0:T(128)S(1)}, s32[4]{0:T(128)S(1)}, u32[]{:S(2)}, u32[]{:S(2)}) collective-permute-start(s32[4]{0:T(128)S(1)} %get-tuple-element.57), channel_id=1, source_target_pairs={{0,8},{4,12},{8,0},{12,4},{1,9},{5,13},{9,1},{13,5},{2,10},{6,14},... | collective-permute-start | bytes 56 | tf_op jit(solution)/shard_map/ppermute | solution.py:468
  8.8 57.3 %collective-permute-start = (s32[4]{0:T(128)S(1)}, s32[4]{0:T(128)S(1)}, u32[]{:S(2)}, u32[]{:S(2)}) collective-permute-start(s32[4]{0:T(128)S(1)} %get-tuple-element.58), channel_id=1, source_target_pairs={{0,4},{4,8},{8,12},{12,0},{1,5},{5,9},{9,13},{13,1},{2,6},{6,10},{... | collective-permute-start | bytes 56 | tf_op jit(solution)/shard_map/ppermute | solution.py:468
  12.8 0.7 copy-start.17
  13.5 46.4 %copy-start.19 = (f32[16]{0:T(128)S(1)}, f32[16]{0:T(128)}, u32[]{:S(2)}) copy-start(f32[16]{0:T(128)} %param.16) | copy-start | bytes 196
  39.6 43.0 %collective-permute-start.5 = (f32[2,2,128,128]{3,2,1,0:T(8,128)}, f32[2,2,128,128]{3,2,1,0:T(8,128)S(1)}, u32[]{:S(2)}, u32[]{:S(2)}) collective-permute-start(f32[2,2,128,128]{3,2,1,0:T(8,128)} %bitcast.62), channel_id=1, source_target_pairs={{0,1},{1,0},{2,3},{3,2},{4,5},{5,4},{6,7},{7,6},{8,9},{9,8},{10,11... | collective-permute-start | bytes 786440 | tf_op jit(solution)/shard_map/ppermute | solution.py:460
  57.4 12.5 %collective-permute-start.7 = (bf16[4,128,128]{2,1,0:T(8,128)(2,1)}, bf16[4,128,128]{2,1,0:T(8,128)(2,1)S(1)}, u32[]{:S(2)}, u32[]{:S(2)}) collective-permute-start(bf16[4,128,128]{2,1,0:T(8,128)(2,1)} %get-tuple-element.18), channel_id=1, source_target_pairs={{0,4},{4,8},{8,12},{12,0},{1,5},{5,9},{9,13},{13,1},{2,6},{6,10},{... | collective-permute-start | bytes 393224 | tf_op jit(solution)/shard_map/ppermute | solution.py:468
  63.8 9.3 %collective-permute-start.8 = (bf16[4,128,128]{2,1,0:T(8,128)(2,1)}, bf16[4,128,128]{2,1,0:T(8,128)(2,1)S(1)}, u32[]{:S(2)}, u32[]{:S(2)}) collective-permute-start(bf16[4,128,128]{2,1,0:T(8,128)(2,1)} %get-tuple-element.19), channel_id=1, source_target_pairs={{0,8},{4,12},{8,0},{12,4},{1,9},{5,13},{9,1},{13,5},{2,10},{6,14},... | collective-permute-start | bytes 393224 | tf_op jit(solution)/shard_map/ppermute | solution.py:468
  64.7 8.5 %collective-permute-start.9 = (bf16[4,128,128]{2,1,0:T(8,128)(2,1)}, bf16[4,128,128]{2,1,0:T(8,128)(2,1)S(1)}, u32[]{:S(2)}, u32[]{:S(2)}) collective-permute-start(bf16[4,128,128]{2,1,0:T(8,128)(2,1)} %get-tuple-element.20), channel_id=1, source_target_pairs={{0,12},{4,0},{8,4},{12,8},{1,13},{5,1},{9,5},{13,9},{2,14},{6,2},{... | collective-permute-start | bytes 393224 | tf_op jit(solution)/shard_map/ppermute | solution.py:468
  66.9 6.2 %copy-start.18 = (s32[16]{0:T(128)}, s32[16]{0:T(128)S(1)}, u32[]{:S(2)}) copy-start(s32[16]{0:T(128)S(1)} %compare_select_fusion.25.label) | copy-start | bytes 196
  67.2 1.2 collective-permute-start.3
  68.4 9.9 %collective-permute-start.4 = (f32[32]{0:T(128)S(1)}, f32[32]{0:T(128)S(1)}, u32[]{:S(2)}, u32[]{:S(2)}) collective-permute-start(f32[32]{0:T(128)S(1)} %bitcast_add_fusion), channel_id=1, source_target_pairs={{0,2},{1,3},{2,0},{3,1},{4,6},{5,7},{6,4},{7,5},{8,10},{9,11},{10,... | collective-permute-start | bytes 392 | tf_op jit(solution)/shard_map/ppermute | solution.py:463
  69.9 3.2 %copy-start.9 = (bf16[4,128,128]{2,1,0:T(8,128)(2,1)}, bf16[4,128,128]{2,1,0:T(8,128)(2,1)S(1)}, u32[]{:S(2)}) copy-start(bf16[4,128,128]{2,1,0:T(8,128)(2,1)S(1)} %collective-permute-done.7.refs_1_) | copy-start | bytes 393220
  73.1 0.6 copy-start.10
  73.1 0.7 copy-start.11
  78.3 1.7 collective-permute-start.10
  81.0 5.6 %collective-permute-start.11 = (f32[2,128,128]{2,1,0:T(8,128)S(1)}, f32[2,128,128]{2,1,0:T(8,128)S(1)}, u32[]{:S(2)}, u32[]{:S(2)}) collective-permute-start(f32[2,128,128]{2,1,0:T(8,128)S(1)} %fusion.3), channel_id=1, source_target_pairs={{0,2},{1,3},{2,0},{3,1},{4,6},{5,7},{6,4},{7,5},{8,10},{9,11},{10,... | collective-permute-start | bytes 393224 | tf_op jit(solution)/shard_map/ppermute | solution.py:463
  84.2 5.3 %collective-permute-start.6 = (f32[2,128,128]{2,1,0:T(8,128)S(1)}, f32[2,128,128]{2,1,0:T(8,128)S(1)}, u32[]{:S(2)}, u32[]{:S(2)}) collective-permute-start(f32[2,128,128]{2,1,0:T(8,128)S(1)} %get-tuple-element.39), channel_id=1, source_target_pairs={{0,2},{1,3},{2,0},{3,1},{4,6},{5,7},{6,4},{7,5},{8,10},{9,11},{10,... | collective-permute-start | bytes 393224 | tf_op jit(solution)/shard_map/ppermute | solution.py:463
  89.5 0.7 copy-start.12
  93.0 7.0 %collective-permute-start.14 = (bf16[2,128,128]{2,1,0:T(8,128)(2,1)}, bf16[2,128,128]{2,1,0:T(8,128)(2,1)S(1)}, u32[]{:S(2)}, u32[]{:S(2)}) collective-permute-start(bf16[2,128,128]{2,1,0:T(8,128)(2,1)} %residual_field.2), channel_id=1, source_target_pairs={{0,4},{4,8},{8,12},{12,0},{1,5},{5,9},{9,13},{13,1},{2,6},{6,10},{... | collective-permute-start | bytes 196616 | tf_op jit(solution)/shard_map/ppermute | solution.py:468
  96.2 6.4 %collective-permute-start.13 = (bf16[2,128,128]{2,1,0:T(8,128)(2,1)}, bf16[2,128,128]{2,1,0:T(8,128)(2,1)S(1)}, u32[]{:S(2)}, u32[]{:S(2)}) collective-permute-start(bf16[2,128,128]{2,1,0:T(8,128)(2,1)} %residual_field.2), channel_id=1, source_target_pairs={{0,8},{4,12},{8,0},{12,4},{1,9},{5,13},{9,1},{13,5},{2,10},{6,14},... | collective-permute-start | bytes 196616 | tf_op jit(solution)/shard_map/ppermute | solution.py:468
  97.9 5.0 %collective-permute-start.12 = (bf16[2,128,128]{2,1,0:T(8,128)(2,1)}, bf16[2,128,128]{2,1,0:T(8,128)(2,1)S(1)}, u32[]{:S(2)}, u32[]{:S(2)}) collective-permute-start(bf16[2,128,128]{2,1,0:T(8,128)(2,1)} %residual_field.2), channel_id=1, source_target_pairs={{0,12},{4,0},{8,4},{12,8},{1,13},{5,1},{9,5},{13,9},{2,14},{6,2},{... | collective-permute-start | bytes 196616 | tf_op jit(solution)/shard_map/ppermute | solution.py:468
  103.8 8.3 %copy-start.1 = (bf16[8,128,128]{2,1,0:T(8,128)(2,1)}, bf16[8,128,128]{2,1,0:T(8,128)(2,1)S(1)}, u32[]{:S(2)}) copy-start(bf16[8,128,128]{2,1,0:T(8,128)(2,1)S(1)} %pad_maximum_fusion.refs_0_) | copy-start | bytes 786436
  103.8 6.8 %collective-permute-start.15 = (bf16[8,128,128]{2,1,0:T(8,128)(2,1)S(1)}, bf16[8,128,128]{2,1,0:T(8,128)(2,1)S(1)}, u32[]{:S(2)}, u32[]{:S(2)}) collective-permute-start(bf16[8,128,128]{2,1,0:T(8,128)(2,1)S(1)} %pad_maximum_fusion.refs_0_), channel_id=1, source_target_pairs={{0,2},{1,3},{2,0},{3,1},{4,6},{5,7},{6,4},{7,5},{8,10},{9,11},{10,... | collective-permute-start | bytes 786440 | tf_op jit(solution)/shard_map/ppermute | solution.py:463
  105.5 6.5 %collective-permute-start.16 = (bf16[8,128,128]{2,1,0:T(8,128)(2,1)S(1)}, bf16[8,128,128]{2,1,0:T(8,128)(2,1)S(1)}, u32[]{:S(2)}, u32[]{:S(2)}) collective-permute-start(bf16[8,128,128]{2,1,0:T(8,128)(2,1)S(1)} %pad_maximum_fusion.refs_0_), channel_id=1, source_target_pairs={{0,1},{1,0},{2,3},{3,2},{4,5},{5,4},{6,7},{7,6},{8,9},{9,8},{10,11... | collective-permute-start | bytes 786440 | tf_op jit(solution)/shard_map/ppermute | solution.py:460
  110.5 1.5 copy-start.3
  110.5 1.5 collective-permute-start.17
  111.4 0.7 copy-start.16
  112.0 0.7 copy-start.4
  112.1 0.7 copy-start.6
  136.6 3.1 %collective-permute-start.18 = (f32[2,8,128,128]{3,2,1,0:T(8,128)}, f32[2,8,128,128]{3,2,1,0:T(8,128)S(1)}, u32[]{:S(2)}, u32[]{:S(2)}) collective-permute-start(f32[2,8,128,128]{3,2,1,0:T(8,128)} %bitcast.61), channel_id=1, source_target_pairs={{0,1},{1,0},{2,3},{3,2},{4,5},{5,4},{6,7},{7,6},{8,9},{9,8},{10,11... | collective-permute-start | bytes 3145736 | tf_op jit(solution)/shard_map/ppermute | solution.py:460
  140.8 14.3 %collective-permute-start.19 = (f32[8,128,128]{2,1,0:T(8,128)S(1)}, f32[8,128,128]{2,1,0:T(8,128)S(1)}, u32[]{:S(2)}, u32[]{:S(2)}) collective-permute-start(f32[8,128,128]{2,1,0:T(8,128)S(1)} %fusion), channel_id=1, source_target_pairs={{0,2},{1,3},{2,0},{3,1},{4,6},{5,7},{6,4},{7,5},{8,10},{9,11},{10,... | collective-permute-start | bytes 1572872 | tf_op jit(solution)/shard_map/ppermute | solution.py:463
  156.9 5.8 %collective-permute-start.22 = (f32[2,128,128]{2,1,0:T(8,128)S(1)}, f32[2,128,128]{2,1,0:T(8,128)S(1)}, u32[]{:S(2)}, u32[]{:S(2)}) collective-permute-start(f32[2,128,128]{2,1,0:T(8,128)S(1)} %get-tuple-element.35), channel_id=1, source_target_pairs={{0,12},{4,0},{8,4},{12,8},{1,13},{5,1},{9,5},{13,9},{2,14},{6,2},{... | collective-permute-start | bytes 393224 | tf_op jit(solution)/shard_map/ppermute | solution.py:468
  158.8 12.9 %collective-permute-start.21 = (f32[2,128,128]{2,1,0:T(8,128)S(1)}, f32[2,128,128]{2,1,0:T(8,128)S(1)}, u32[]{:S(2)}, u32[]{:S(2)}) collective-permute-start(f32[2,128,128]{2,1,0:T(8,128)S(1)} %get-tuple-element.36), channel_id=1, source_target_pairs={{0,8},{4,12},{8,0},{12,4},{1,9},{5,13},{9,1},{13,5},{2,10},{6,14},... | collective-permute-start | bytes 393224 | tf_op jit(solution)/shard_map/ppermute | solution.py:468
  160.4 11.3 %collective-permute-start.20 = (f32[2,128,128]{2,1,0:T(8,128)S(1)}, f32[2,128,128]{2,1,0:T(8,128)S(1)}, u32[]{:S(2)}, u32[]{:S(2)}) collective-permute-start(f32[2,128,128]{2,1,0:T(8,128)S(1)} %get-tuple-element.37), channel_id=1, source_target_pairs={{0,4},{4,8},{8,12},{12,0},{1,5},{5,9},{9,13},{13,1},{2,6},{6,10},{... | collective-permute-start | bytes 393224 | tf_op jit(solution)/shard_map/ppermute | solution.py:468
  162.7 9.0 %copy-start.13 = (f32[2,128,128]{2,1,0:T(8,128)}, f32[2,128,128]{2,1,0:T(8,128)S(1)}, u32[]{:S(2)}) copy-start(f32[2,128,128]{2,1,0:T(8,128)S(1)} %collective-permute-done.22.refs_3_) | copy-start | bytes 393220
  171.7 0.7 copy-start.14
  171.7 0.7 copy-start.15
  175.4 6.5 %collective-permute-start.25 = (bf16[2,128,128]{2,1,0:T(8,128)(2,1)}, bf16[2,128,128]{2,1,0:T(8,128)(2,1)S(1)}, u32[]{:S(2)}, u32[]{:S(2)}) collective-permute-start(bf16[2,128,128]{2,1,0:T(8,128)(2,1)} %residual_field.3), channel_id=1, source_target_pairs={{0,4},{4,8},{8,12},{12,0},{1,5},{5,9},{9,13},{13,1},{2,6},{6,10},{... | collective-permute-start | bytes 196616 | tf_op jit(solution)/shard_map/ppermute | solution.py:468
  175.4 7.7 %collective-permute-start.24 = (bf16[2,128,128]{2,1,0:T(8,128)(2,1)}, bf16[2,128,128]{2,1,0:T(8,128)(2,1)S(1)}, u32[]{:S(2)}, u32[]{:S(2)}) collective-permute-start(bf16[2,128,128]{2,1,0:T(8,128)(2,1)} %residual_field.3), channel_id=1, source_target_pairs={{0,8},{4,12},{8,0},{12,4},{1,9},{5,13},{9,1},{13,5},{2,10},{6,14},... | collective-permute-start | bytes 196616 | tf_op jit(solution)/shard_map/ppermute | solution.py:468
  176.1 6.9 %collective-permute-start.23 = (bf16[2,128,128]{2,1,0:T(8,128)(2,1)}, bf16[2,128,128]{2,1,0:T(8,128)(2,1)S(1)}, u32[]{:S(2)}, u32[]{:S(2)}) collective-permute-start(bf16[2,128,128]{2,1,0:T(8,128)(2,1)} %residual_field.3), channel_id=1, source_target_pairs={{0,12},{4,0},{8,4},{12,8},{1,13},{5,1},{9,5},{13,9},{2,14},{6,2},{... | collective-permute-start | bytes 196616 | tf_op jit(solution)/shard_map/ppermute | solution.py:468
  183.9 8.0 %copy-start.2 = (bf16[8,128,128]{2,1,0:T(8,128)(2,1)}, bf16[8,128,128]{2,1,0:T(8,128)(2,1)S(1)}, u32[]{:S(2)}) copy-start(bf16[8,128,128]{2,1,0:T(8,128)(2,1)S(1)} %pad_maximum_fusion.1.refs_0_) | copy-start | bytes 786436
  183.9 6.4 %collective-permute-start.26 = (bf16[8,128,128]{2,1,0:T(8,128)(2,1)S(1)}, bf16[8,128,128]{2,1,0:T(8,128)(2,1)S(1)}, u32[]{:S(2)}, u32[]{:S(2)}) collective-permute-start(bf16[8,128,128]{2,1,0:T(8,128)(2,1)S(1)} %pad_maximum_fusion.1.refs_0_), channel_id=1, source_target_pairs={{0,2},{1,3},{2,0},{3,1},{4,6},{5,7},{6,4},{7,5},{8,10},{9,11},{10,... | collective-permute-start | bytes 786440 | tf_op jit(solution)/shard_map/ppermute | solution.py:463
  185.7 4.6 %collective-permute-start.27 = (bf16[8,128,128]{2,1,0:T(8,128)(2,1)S(1)}, bf16[8,128,128]{2,1,0:T(8,128)(2,1)S(1)}, u32[]{:S(2)}, u32[]{:S(2)}) collective-permute-start(bf16[8,128,128]{2,1,0:T(8,128)(2,1)S(1)} %pad_maximum_fusion.1.refs_0_), channel_id=1, source_target_pairs={{0,1},{1,0},{2,3},{3,2},{4,5},{5,4},{6,7},{7,6},{8,9},{9,8},{10,11... | collective-permute-start | bytes 786440 | tf_op jit(solution)/shard_map/ppermute | solution.py:460
  190.4 1.5 copy-start.5
  190.4 1.5 collective-permute-start.28
  190.4 1.5 copy-start.7
  191.9 0.7 copy-start.8

commit v2 on v1

--- a/solution.py
+++ b/solution.py
@@ -12,7 +12,8 @@
 AMP_CONTRAST = 0.1
 PHASE_RATE = 60.0
 BLOCK = 16
-WINDOW = 24
+WINDOW = 16
+LANES = 128
 SMEM = pltpu.SMEM
 
 
@@ -67,67 +68,66 @@
     y_edge = y_part + jnp.minimum(0.0, (BLOCK - 1) * cosine)[None, :]
     z_edge = z_part + jnp.minimum(0.0, (BLOCK - 1) * sine)[None, :]
     least = y_edge[:, None, :] + z_edge[None, :, :]
-    column = jnp.floor((least - 3.0 + middle) / 16.0).astype(jnp.int32) * 8
+    column = jnp.floor((least - 3.0 + middle) / 2.0).astype(jnp.int32)
     start = jnp.clip(column, 0, image_side - WINDOW)
     offset = scale * (
         y_part[:, None, :] + z_part[None, :, :] - (2.0 * start.astype(jnp.float32) + 1.0 - middle)
     )
     direction = jnp.stack([cosine, sine]) * scale
-    return direction.reshape(-1), start.reshape(-1), offset.reshape(-1)
-
-
-def local_tables(map_side):
+    blocks = row_blocks * plane_blocks
+    lanes = offset.reshape(blocks, 1, -1, 1) - 2.0 * scale * jnp.arange(
+        WINDOW, dtype=jnp.float32
+    )
+    wide = jnp.repeat(direction, WINDOW, axis=1)
+    return (
+        (direction.reshape(-1), start.reshape(-1), offset.reshape(-1)),
+        (wide, lanes.reshape(blocks, 1, -1)),
+    )
+
+
+def fill_windows(w_ref, direction, offset, block, poses, map_side):
     lane = lax.broadcasted_iota(jnp.int32, (8, BLOCK * BLOCK), 1)
     row = lax.broadcasted_iota(jnp.int32, (8, BLOCK * BLOCK), 0).astype(jnp.float32)
     y_local = (lane // BLOCK).astype(jnp.float32)
     z_local = (lane % BLOCK).astype(jnp.float32)
-    scale = 0.25 / math.sqrt(map_side)
-    rows = [(2.0 * scale) * (row + 8.0 * k) for k in range(WINDOW // 8)]
-    return y_local, z_local, rows
-
-
-def make_window(tables, direction, offset, pose, base, poses, map_side):
-    y_local, z_local, rows = tables
     peak = 0.5 / math.sqrt(map_side)
-    line = y_local * direction[pose] + z_local * direction[poses + pose] + offset[base + pose]
-    return [jnp.maximum(0.0, peak - jnp.abs(line - r)) for r in rows]
-
-
-def fill_windows(w_ref, tables, direction, offset, block, poses, map_side):
+    rows = [peak * (row + 8.0 * k) for k in range(WINDOW // 8)]
     base = block * poses
-
-    def pair(k, _):
-        parts = []
-        for half in range(2):
-            parts += make_window(
-                tables, direction, offset, 2 * k + half, base, poses, map_side
-            )
-        at = pl.multiple_of(k * 2 * WINDOW, 2 * WINDOW)
-        w_ref[pl.ds(at, 2 * WINDOW), :] = jnp.concatenate(parts, axis=0).astype(jnp.bfloat16)
-        return 0
-
-    lax.fori_loop(0, poses // 2, pair, 0, unroll=min(8, poses // 2))
-
-
-def add_projection(outs, prod_ref, start, block, poses):
+    for pose in range(poses):
+        line = (
+            y_local * direction[pose] + z_local * direction[poses + pose] + offset[base + pose]
+        )
+        parts = [jnp.maximum(0.0, peak - jnp.abs(line - r)) for r in rows]
+        w_ref[pose * WINDOW : (pose + 1) * WINDOW, :] = jnp.concatenate(parts, axis=0).astype(
+            jnp.bfloat16
+        )
+
+
+def fill_turned(t_ref, wide, lanes, block, map_side):
+    peak = 0.5 / math.sqrt(map_side)
+    local = lax.broadcasted_iota(jnp.int32, (BLOCK, LANES), 0).astype(jnp.float32)
+    offset = lanes[block]
+    for at in range(0, wide.shape[1], LANES):
+        span = slice(at, at + LANES)
+        along_z = local * wide[1:2, span] + offset[:, span]
+        along_y = wide[0:1, span]
+        for y in range(BLOCK):
+            line = along_z + float(y) * along_y
+            t_ref[y * BLOCK : (y + 1) * BLOCK, span] = jnp.maximum(
+                0.0, peak - jnp.abs(line)
+            ).astype(jnp.bfloat16)
+
+
+def add_projection(outs, prod, start, block, poses):
     base = block * poses
     share = poses // len(outs)
-
-    for part, out in enumerate(outs):
-
-        def one(k, _, part=part, out=out):
-            pose = part * share + k
-            at = pl.multiple_of(start[base + pose], 8)
-            rows = pl.multiple_of(pose * WINDOW, 8)
-            out[k, pl.ds(at, WINDOW), :] += prod_ref[pl.ds(rows, WINDOW), :]
-            return 0
-
-        lax.fori_loop(0, share, one, 0, unroll=min(8, share))
+    for pose in range(poses):
+        rows = pl.ds(start[base + pose], WINDOW)
+        outs[pose // share][pose % share, rows, :] += prod[pose * WINDOW : (pose + 1) * WINDOW]
 
 
 def first_projection_kernel(
-    map_side, poses, plane_blocks, row_blocks, direction, start, offset, dens, pool_t, keep, send,
-    w_ref, prod_ref
+    map_side, poses, direction, start, offset, dens, pool_t, keep, send, fold_ref, w_ref
 ):
     step = pl.program_id(0)
 
@@ -136,57 +136,48 @@
         keep[...] = jnp.zeros_like(keep)
         send[...] = jnp.zeros_like(send)
 
-    tables = local_tables(map_side)
-
-    def block(k, _):
-        row, plane = k // plane_blocks, k % plane_blocks
-        rows = pl.ds(pl.multiple_of(row * BLOCK, BLOCK), BLOCK)
-        planes = pl.ds(pl.multiple_of(plane * BLOCK, BLOCK), BLOCK)
-        values = dens[rows, planes, :].reshape(BLOCK * BLOCK, map_side)
-        folded = jnp.dot(values, pool_t[...], preferred_element_type=jnp.float32)
-        index = step * row_blocks * plane_blocks + k
-        fill_windows(w_ref, tables, direction, offset, index, poses, map_side)
-        prod_ref[...] = jnp.dot(
-            w_ref[...], folded.astype(jnp.bfloat16), preferred_element_type=jnp.float32
-        )
-        add_projection((keep, send), prod_ref, start, index, poses)
-        return 0
-
-    lax.fori_loop(0, row_blocks * plane_blocks, block, 0)
+    height, depth, _ = dens.shape
+    side = pool_t.shape[1]
+    folded = jnp.dot(
+        dens[...].reshape(height * depth, map_side), pool_t[...], preferred_element_type=jnp.float32
+    )
+    fold_ref[...] = folded.astype(jnp.bfloat16).reshape(height, depth, side)
+    count = height * depth // (BLOCK * BLOCK)
+    for k in range(count):
+        row, plane = k // (depth // BLOCK) * BLOCK, k % (depth // BLOCK) * BLOCK
+        weights = w_ref.at[k % 2]
+        fill_windows(weights, direction, offset, step * count + k, poses, map_side)
+        pixels = fold_ref[row : row + BLOCK, plane : plane + BLOCK, :].reshape(-1, side)
+        prod = jnp.dot(weights[...], pixels, preferred_element_type=jnp.float32)
+        add_projection((keep, send), prod, start, step * count + k, poses)
 
 
 def first_projection(density, pool_t, geo, poses):
     map_side, depth, _ = density.shape
     side = pool_t.shape[1]
-    row_blocks = 2
+    height = 2 * BLOCK
     half = jax.ShapeDtypeStruct((poses // 2, side, side), jnp.float32)
     return pl.pallas_call(
-        functools.partial(first_projection_kernel, map_side, poses, depth // BLOCK, row_blocks),
-        grid=(map_side // (BLOCK * row_blocks),),
+        functools.partial(first_projection_kernel, map_side, poses),
+        grid=(map_side // height,),
         in_specs=[smem(), smem(), smem(),
-                  pl.BlockSpec((BLOCK * row_blocks, depth, map_side), lambda i: (i, 0, 0)),
+                  pl.BlockSpec((height, depth, map_side), lambda i: (i, 0, 0)),
                   vmem()],
         out_specs=[vmem(), vmem()],
         out_shape=[half, half],
         scratch_shapes=[
-            pltpu.VMEM((poses * WINDOW, BLOCK * BLOCK), jnp.bfloat16),
-            pltpu.VMEM((poses * WINDOW, side), jnp.float32),
+            pltpu.VMEM((height, depth, side), jnp.bfloat16),
+            pltpu.VMEM((2, poses * WINDOW, BLOCK * BLOCK), jnp.bfloat16),
         ],
         name="first_projection",
     )(*geo, density, pool_t)
 
 
-def pick_kernel(count, order, images, *rest):
-    outs, sems = rest[:-1], rest[-1]
-    each = count // len(outs)
-    copies = [
-        pltpu.make_async_copy(images.at[order[k]], outs[k // each].at[k % each], sems.at[k])
-        for k in range(count)
-    ]
-    for copy in copies:
-        copy.start()
-    for copy in copies:
-        copy.wait()
+def pick_kernel(order, images, *outs):
+    each = outs[0].shape[0]
+    for group, out in enumerate(outs):
+        for k in range(each):
+            out[k] = images[order[group * each + k]]
 
 
 def pick_images(images, order, groups):
@@ -194,11 +185,10 @@
     _, side, _ = images.shape
     out = jax.ShapeDtypeStruct((count // groups, side, side), images.dtype)
     return pl.pallas_call(
-        functools.partial(pick_kernel, count),
-        in_specs=[smem(), pl.BlockSpec(memory_space=pl.ANY)],
-        out_specs=[pl.BlockSpec(memory_space=pl.ANY)] * groups,
+        pick_kernel,
+        in_specs=[smem(), vmem()],
+        out_specs=[vmem()] * groups,
         out_shape=[out] * groups,
-        scratch_shapes=[pltpu.SemaphoreType.DMA((count,))],
         name="pick_images",
     )(order, images)
 
@@ -303,23 +293,14 @@
 
 def gather_windows(f_ref, field, start, block, poses):
     base = block * poses
-
-    def pair(k, _):
-        parts = []
-        for half in range(2):
-            at = pl.multiple_of(start[base + 2 * k + half], 8)
-            parts.append(field[2 * k + half, pl.ds(at, WINDOW), :])
-        rows = pl.multiple_of(k * 2 * WINDOW, 2 * WINDOW)
-        f_ref[pl.ds(rows, 2 * WINDOW), :] = jnp.concatenate(parts, axis=0).astype(jnp.bfloat16)
-        return 0
-
-    lax.fori_loop(0, poses // 2, pair, 0, unroll=min(8, poses // 2))
-
-
-def block_gradient(w_ref, f_ref, pool2):
-    back = lax.dot_general(
-        w_ref[...], f_ref[...], (((0,), (0,)), ((), ())), preferred_element_type=jnp.float32
-    )
+    for pose in range(poses):
+        f_ref[pose * WINDOW : (pose + 1) * WINDOW, :] = field[
+            pose, pl.ds(start[base + pose], WINDOW), :
+        ].astype(jnp.bfloat16)
+
+
+def block_gradient(t_ref, f_ref, pool2):
+    back = jnp.dot(t_ref[...], f_ref[...], preferred_element_type=jnp.float32)
     high = back.astype(jnp.bfloat16)
     low = (back - high.astype(jnp.float32)).astype(jnp.bfloat16)
     return jnp.dot(
@@ -328,11 +309,11 @@
 
 
 def step_kernel(
-    map_side, poses, plane_blocks, parts, bin_ref, direction, start, offset, sizes, dens, pool2,
+    map_side, poses, parts, bin_ref, direction, start, offset, sizes, dens, wide, lanes, pool2,
     pool_t, *refs
 ):
     fields = refs[:parts]
-    first, keep, send, field, w_ref, f_ref, prod_ref = refs[parts:]
+    first, keep, send, field, t_ref, w_ref, f_ref = refs[parts:]
     step = pl.program_id(0)
 
     @pl.when(step == 0)
@@ -341,101 +322,93 @@
         send[...] = jnp.zeros_like(send)
         load_fields(field, fields)
 
-    tables = local_tables(map_side)
-
-    def block(k, _):
-        planes = pl.ds(pl.multiple_of(k * BLOCK, BLOCK), BLOCK)
-        index = step * plane_blocks + k
-        fill_windows(w_ref, tables, direction, offset, index, poses, map_side)
-        gather_windows(f_ref, field, start, index, poses)
-        grad = block_gradient(w_ref, f_ref, pool2)
+    count = dens.shape[1] // BLOCK
+    for k in range(count):
+        planes = slice(k * BLOCK, (k + 1) * BLOCK)
+        index = step * count + k
+        turned, weights, windows = t_ref.at[k % 2], w_ref.at[k % 2], f_ref.at[k % 2]
+        fill_turned(turned, wide, lanes, index, map_side)
+        gather_windows(windows, field, start, index, poses)
+        grad = block_gradient(turned, windows, pool2)
         values = dens[:, planes, :].reshape(BLOCK * BLOCK, map_side).astype(jnp.float32)
         moved = values - sizes[0] * grad
         first[:, planes, :] = moved.reshape(BLOCK, BLOCK, map_side)
         folded = jnp.dot(
             moved.astype(jnp.bfloat16), pool_t[...], preferred_element_type=jnp.float32
         )
-        prod_ref[...] = jnp.dot(
-            w_ref[...], folded.astype(jnp.bfloat16), preferred_element_type=jnp.float32
+        fill_windows(weights, direction, offset, index, poses, map_side)
+        prod = jnp.dot(
+            weights[...], folded.astype(jnp.bfloat16), preferred_element_type=jnp.float32
         )
-        add_projection((keep, send), prod_ref, start, index, poses)
-        return 0
-
-    lax.fori_loop(0, plane_blocks, block, 0)
-
-
-def take_step(density, fields, geo, sizes, bin_index, pool2, pool_t, poses, row_share):
+        add_projection((keep, send), prod, start, index, poses)
+
+
+def take_step(density, fields, geo, wide_geo, sizes, bin_index, pool2, pool_t, poses, row_share):
     map_side, depth, _ = density.shape
     side = pool_t.shape[1]
     half = jax.ShapeDtypeStruct((poses // 2, side, side), jnp.float32)
     row_blocks = row_share // BLOCK
     rows = (BLOCK, depth, map_side)
-    scalars = (geo[0], geo[1], geo[2], sizes)
     return pl.pallas_call(
-        functools.partial(step_kernel, map_side, poses, depth // BLOCK, len(fields)),
+        functools.partial(step_kernel, map_side, poses, len(fields)),
         grid_spec=pltpu.PrefetchScalarGridSpec(
             num_scalar_prefetch=1,
             grid=(row_blocks,),
-            in_specs=[smem()] * len(scalars)
+            in_specs=[smem()] * 4
             + [pl.BlockSpec(rows, lambda i, at: (at[0] * row_blocks + i, 0, 0))]
-            + [vmem()] * (2 + len(fields)),
+            + [vmem()] * (4 + len(fields)),
             out_specs=[pl.BlockSpec(rows, lambda i, at: (i, 0, 0)), vmem(), vmem()],
             scratch_shapes=[
                 pltpu.VMEM((poses, side, side), jnp.float32),
-                pltpu.VMEM((poses * WINDOW, BLOCK * BLOCK), jnp.bfloat16),
-                pltpu.VMEM((poses * WINDOW, side), jnp.bfloat16),
-                pltpu.VMEM((poses * WINDOW, side), jnp.float32),
+                pltpu.VMEM((2, BLOCK * BLOCK, poses * WINDOW), jnp.bfloat16),
+                pltpu.VMEM((2, poses * WINDOW, BLOCK * BLOCK), jnp.bfloat16),
+                pltpu.VMEM((2, poses * WINDOW, side), jnp.bfloat16),
             ],
         ),
         out_shape=[jax.ShapeDtypeStruct((row_share, depth, map_side), jnp.float32), half, half],
         name="take_step",
-    )(bin_index.reshape(1), *scalars, density, pool2, pool_t, *fields)
-
-
-def finish_kernel(
-    map_side, poses, plane_blocks, parts, direction, start, offset, sizes, first, pool2, *refs
-):
+    )(bin_index.reshape(1), *geo, sizes, density, *wide_geo, pool2, pool_t, *fields)
+
+
+def finish_kernel(map_side, poses, parts, start, sizes, first, wide, lanes, pool2, *refs):
     fields = refs[:parts]
-    gradient, refined, field, w_ref, f_ref = refs[parts:]
+    gradient, refined, field, t_ref, f_ref = refs[parts:]
     step = pl.program_id(0)
 
     @pl.when(step == 0)
     def _():
         load_fields(field, fields)
 
-    tables = local_tables(map_side)
-
-    def block(k, _):
-        planes = pl.ds(pl.multiple_of(k * BLOCK, BLOCK), BLOCK)
-        index = step * plane_blocks + k
-        fill_windows(w_ref, tables, direction, offset, index, poses, map_side)
-        gather_windows(f_ref, field, start, index, poses)
-        grad = block_gradient(w_ref, f_ref, pool2).reshape(BLOCK, BLOCK, map_side)
+    count = first.shape[1] // BLOCK
+    for k in range(count):
+        planes = slice(k * BLOCK, (k + 1) * BLOCK)
+        index = step * count + k
+        turned, windows = t_ref.at[k % 2], f_ref.at[k % 2]
+        fill_turned(turned, wide, lanes, index, map_side)
+        gather_windows(windows, field, start, index, poses)
+        grad = block_gradient(turned, windows, pool2).reshape(BLOCK, BLOCK, map_side)
         gradient[:, planes, :] = grad
         refined[:, planes, :] = first[:, planes, :] - sizes[1] * grad
-        return 0
-
-    lax.fori_loop(0, plane_blocks, block, 0)
-
-
-def finish(first, fields, geo, sizes, pool2, poses):
+
+
+def finish(first, fields, geo, wide_geo, sizes, pool2, poses):
     row_share, depth, map_side = first.shape
     side = pool2.shape[0] // 2
     rows = pl.BlockSpec((BLOCK, depth, map_side), lambda i: (i, 0, 0))
     out = jax.ShapeDtypeStruct(first.shape, jnp.float32)
     return pl.pallas_call(
-        functools.partial(finish_kernel, map_side, poses, depth // BLOCK, len(fields)),
+        functools.partial(finish_kernel, map_side, poses, len(fields)),
         grid=(row_share // BLOCK,),
-        in_specs=[smem()] * 4 + [rows] + [vmem()] * (1 + len(fields)),
+        in_specs=[smem()] * 2 + [rows] + [vmem()] * (3 + len(fields)),
         out_specs=[rows, rows],
         out_shape=[out, out],
         scratch_shapes=[
             pltpu.VMEM((poses, side, side), jnp.float32),
-            pltpu.VMEM((poses * WINDOW, BLOCK * BLOCK), jnp.bfloat16),
-            pltpu.VMEM((poses * WINDOW, side), jnp.bfloat16),
+            pltpu.VMEM((2, BLOCK * BLOCK, poses * WINDOW), jnp.bfloat16),
+            pltpu.VMEM((2, poses * WINDOW, side), jnp.bfloat16),
         ],
         name="finish",
-    )(*geo, sizes, first, pool2, *fields)
+    )(geo[1], sizes, first, *wide_geo, pool2, *fields)
 
 
 def on_device(
@@ -482,10 +455,10 @@
     rel = rel.reshape(bins, 2, chips, owned).transpose(1, 2, 0, 3).reshape(-1)
     poses = bins * pose_count
     first_plane = slab_index * depth
-    own_geo = geometry(
+    own_geo, _ = geometry(
         own_angles, 0, map_side // BLOCK, first_plane, depth // BLOCK, side, map_side
     )
-    geo = geometry(
+    geo, wide_geo = geometry(
         rel, bin_index * row_share, row_share // BLOCK, first_plane, depth // BLOCK, side, map_side
     )
     pooling = pool_table(side, map_side).astype(jnp.bfloat16)
@@ -505,6 +478,7 @@
     mark = image_pose * classes + image_class + 1
     marks = jnp.sum(jnp.where(placement, mark[None, :], 0), axis=1) - 1
     picked = pick_images(images, order, bins)
+    picked, own_geo = lax.optimization_barrier((picked, own_geo))
     marks = marks.reshape(bins, capacity)
     got_images = [picked[0]] + [to_bin(picked[d], d) for d in range(1, bins)]
     got_marks = [marks[0]] + [to_bin(marks[d], d) for d in range(1, bins)]
@@ -546,13 +520,14 @@
 
     field = residual_field(proj_parts, total, tally, ctf, table, weight)
     first, keep, send = take_step(
-        density, share_field(field), geo, step_sizes, bin_index, pool2, pool_t, poses, row_share
+        density, share_field(field), geo, wide_geo, step_sizes, bin_index, pool2, pool_t, poses,
+        row_share,
     )
     parts = functools.reduce(jnp.add, reduce_slab(split(keep), split(send)))
     parts = parts.reshape(bins, owned, side, side)
     parts = [parts[0]] + [to_bin(parts[d], d) for d in range(1, bins)]
     field = residual_field(parts, total, tally, ctf, table, weight)
-    gradient, refined = finish(first, share_field(field), geo, step_sizes, pool2, poses)
+    gradient, refined = finish(first, share_field(field), geo, wide_geo, step_sizes, pool2, poses)
     return (gradient, refined)
 
 

time: 208 us -> 158 us (0.76)
  Pallas kernels: 92.4 us -> 44.8 us
  waiting for transfers between devices: 54.4 us -> 51 us
    pallas_call x3, Pallas kernels: 56.2 us -> 24.4 us  [the longest x1 13.3 us: take_step(): pl.pallas_call(functools.partial(step_kernel, map_side, poses, len(fields...]
    pallas_call x1, Pallas kernels: 26 us -> 10.2 us  [first_projection(): pl.pallas_call(functools.partial(first_projection_kernel, map_side, poses...]
    ppermute x15, waiting for transfers between devices: 22.6 us -> 19.2 us  [to_bin(): lax.ppermute(value, 'bin', [(b, (b + shift) % bins) for b in range(bins)])]
  transfers between devices with their start and end apart: 29 -> 29, of which waited for: 18 -> 15; matrix products, arithmetic and copies ran while one was open for 7% -> 11% of each run, Pallas kernels for 23% -> 11%
where the time goes in v2:
time: 158 us; the launch traced here: 157 us
  waiting for transfers between devices  51 us (32%)
  Pallas kernels  44.8 us (28%)
  starting transfers between devices  31.4 us (20%)
  other arithmetic  17.7 us (11%)
  local copies, waits for them, and re-layouts  11.3 us (7%)
    ppermute x6, waiting for transfers between devices, to_chip(): lax.ppermute(value, 'slab', [(s, (s + 2 * shift) % slabs) for s in range(...  26 us
    ppermute x15, starting transfers between devices, to_bin(): lax.ppermute(value, 'bin', [(b, (b + shift) % bins) for b in range(bins)])  23.2 us
    ppermute x15, waiting for transfers between devices, to_bin(): lax.ppermute(value, 'bin', [(b, (b + shift) % bins) for b in range(bins)])  19.2 us
    pallas_call x1, Pallas kernels, take_step(): pl.pallas_call(functools.partial(step_kernel, map_side, poses, len(fields...  13.3 us
    pallas_call x1, Pallas kernels, first_projection(): pl.pallas_call(functools.partial(first_projection_kernel, map_side, poses...  10.2 us
    pallas_call x1, Pallas kernels, finish(): pl.pallas_call(functools.partial(finish_kernel, map_side, poses, len(fiel...  9.23 us
    ppermute x6, starting transfers between devices, to_chip(): lax.ppermute(value, 'slab', [(s, (s + 2 * shift) % slabs) for s in range(...  7.03 us
    ppermute x8, waiting for transfers between devices, to_core(): return lax.ppermute(value, 'slab', [(s, s ^ 1) for s in range(slabs)])  5.85 us
  transfers between devices with their start and end apart: 29, of which 15 were waited for; matrix products, arithmetic and copies ran while one was open for 11% of the time, Pallas kernels for 11%

profile of v2, /device:TPU:0, one launch (start us, length us, event | category | flops | bytes accessed | tf_op | source)
XLA Modules:
  0.0 157.2 jit_solution(14783156925162964854)
XLA Ops:
  0.7 0.7 fusion.10
  1.4 0.8 select_reduce_fusion.2
  2.3 0.7 fusion.19
  3.0 0.6 select_reduce_fusion
  3.7 5.1 %collective-permute-start.2 = (s32[4]{0:T(128)S(1)}, s32[4]{0:T(128)S(1)}, u32[]{:S(2)}, u32[]{:S(2)}) collective-permute-start(s32[4]{0:T(128)S(1)} %get-tuple-element.72), channel_id=1, source_target_pairs={{0,12},{4,0},{8,4},{12,8},{1,13},{5,1},{9,5},{13,9},{2,14},{6,2},{... | collective-permute-start | bytes 56 | tf_op jit(solution)/shard_map/ppermute | solution.py:441
  8.7 1.0 collective-permute-start
  10.8 0.6 gather_fusion.2
  11.6 0.6 mul.406.direction
  12.7 0.6 subtract_multiply_fusion.1.offset
  13.3 1.9 %pick_images.1 = (bf16[4,128,128]{2,1,0:T(8,128)(2,1)}, bf16[4,128,128]{2,1,0:T(8,128)(2,1)}, bf16[4,128,128]{2,1,0:T(8,128)(2,1)}, bf16[4,128,128]{2,1,0:T(8,128)(2,1)}) custom-call(s32[16]{0:T(128)} %get-tuple-element.40.order, bf16[16,128,128]{2,1,0:T(8,128)(2,1)} %images.1), custom_call_target="tpu_custom_call" | custom-call | tf_op jit(solution)/shard_map/pick_images/pallas_call | solution.py:187
  15.1 2.5 %collective-permute-start.7 = (bf16[4,128,128]{2,1,0:T(8,128)(2,1)}, bf16[4,128,128]{2,1,0:T(8,128)(2,1)S(1)}, u32[]{:S(2)}, u32[]{:S(2)}) collective-permute-start(bf16[4,128,128]{2,1,0:T(8,128)(2,1)} %get-tuple-element.32), channel_id=1, source_target_pairs={{0,4},{4,8},{8,12},{12,0},{1,5},{5,9},{9,13},{13,1},{2,6},{6,10},{... | collective-permute-start | bytes 393224 | tf_op jit(solution)/shard_map/ppermute | solution.py:441
  17.6 0.9 collective-permute-start.8
  18.6 0.7 broadcast_multiply_fusion.4
  21.4 1.6 %add_negate_fusion.ctf = f32[16,128,128]{2,1,0:T(8,128)} fusion(f32[16,128]{1,0:T(8,128)S(1)} %get-tuple-element.64, f32[16,128]{1,0:T(8,128)S(1)} %get-tuple-element.66, f32[16,128]{1,0:T(8,128)S(1)} %get-tuple-element.65, f32[16,128]{1,0:T(8,128)S(1)} %get-tuple-element.63), kind=kLoop, calls=%fused_computation.3 | loop fusion | flops 1048576 | bytes 1081344 | tf_op jit(solution)/shard_map/neg | solution.py:54
  23.0 10.2 %first_projection.1 = (f32[4,128,128]{2,1,0:T(8,128)}, f32[4,128,128]{2,1,0:T(8,128)}) custom-call(f32[16]{0:T(128)} %mul.406.direction, s32[512]{0:T(512)} %copy-done.17, f32[512]{0:T(512)} %subtract_multiply_fusion.1.offset, bf16[256,64,256]{2,1,0:T(8,128)(2,1)} %dens.3, bf16[256,128]{1,0:T(8,128)(2,1)} %constant.237.clone.pool_t), custom_call_target="tpu_custom_call" | custom-call | tf_op jit(solution)/shard_map/first_projection/pallas_call | solution.py:160
  33.2 1.5 collective-permute-start.9
  36.3 0.7 collective-permute-done.3
  37.1 1.5 collective-permute-start.4
  38.6 0.6 copy-done.9
  39.3 0.7 copy-done.11
  39.9 4.5 %image_sums.1 = (f32[4,128,128]{2,1,0:T(8,128)}, f32[4,128,128]{2,1,0:T(8,128)}) custom-call(s32[16]{0:T(128)} %copy-done.18, f32[16,128,128]{2,1,0:T(8,128)} %add_negate_fusion.ctf, bf16[128,256]{1,0:T(8,128)(2,1)} %constant.239.clone.table, bf16[4,128,128]{2,1,0:T(8,128)(2,1)} %get-tuple-element.31.refs_0_, bf16[4,128,128]{2,1,0:T(8,128)(2,1)} %copy-done.9, ...), custom_call_target="tpu_custom_call" | custom-call | tf_op jit(solution)/shard_map/image_sums/pallas_call | solution.py:239
  45.1 1.1 collective-permute-done.10
  46.2 0.9 fusion.3
  47.1 0.6 collective-permute-start.11
  47.7 1.7 %fusion.6 = (f32[2,128,128]{2,1,0:T(8,128)S(1)}, f32[2,128,128]{2,1,0:T(8,128)}) fusion(f32[2,2,128,128]{3,2,1,0:T(8,128)S(1)} %collective-permute-done.5, f32[4,128,128]{2,1,0:T(8,128)} %get-tuple-element.29), kind=kLoop, calls=%fused_computation.17 | loop fusion | flops 65536 | bytes 786432 | tf_op jit(solution)/shard_map/add | solution.py:501
  49.4 1.5 collective-permute-start.6
  50.9 2.7 %collective-permute-done.11 = f32[2,128,128]{2,1,0:T(8,128)S(1)} collective-permute-done((f32[2,128,128]{2,1,0:T(8,128)S(1)}, f32[2,128,128]{2,1,0:T(8,128)S(1)}, u32[]{:S(2)}, u32[]{:S(2)}) %collective-permute-start.11) | collective-permute-done | bytes 131104 | tf_op jit(solution)/shard_map/ppermute | solution.py:436
  53.5 1.6 %fusion.5.refs_2_.refs_4_ = f32[2,128,128]{2,1,0:T(8,128)} fusion(f32[2,128,128]{2,1,0:T(8,128)S(1)} %collective-permute-done.11, f32[2,2,128,128]{3,2,1,0:T(8,128)S(1)} %collective-permute-done.10, f32[4,128,128]{2,1,0:T(8,128)} %get-tuple-element.35), kind=kLoop, calls=%fused_computation.15 | loop fusion | flops 65536 | bytes 524288 | tf_op jit(solution)/shard_map/add | solution.py:513
  55.5 0.7 copy-done.12
  56.2 2.8 %residual_field.2 = bf16[2,128,128]{2,1,0:T(8,128)(2,1)} custom-call(f32[32]{0:T(128)} %fusion.36.tally, f32[16,128,128]{2,1,0:T(8,128)} %add_negate_fusion.ctf, bf16[128,256]{1,0:T(8,128)(2,1)} %constant.239.clone.table, f32[2,128,128]{2,1,0:T(8,128)} %get-tuple-element.54.refs_0_, f32[2,128,128]{2,1,0:T(8,128)} %copy-done.12, ...), custom_call_target="tpu_custom_call" | custom-call | tf_op jit(solution)/shard_map/residual_field/pallas_call | solution.py:277
  59.6 2.3 %collective-permute-start.13 = (bf16[2,128,128]{2,1,0:T(8,128)(2,1)}, bf16[2,128,128]{2,1,0:T(8,128)(2,1)S(1)}, u32[]{:S(2)}, u32[]{:S(2)}) collective-permute-start(bf16[2,128,128]{2,1,0:T(8,128)(2,1)} %residual_field.2), channel_id=1, source_target_pairs={{0,8},{4,12},{8,0},{12,4},{1,9},{5,13},{9,1},{13,5},{2,10},{6,14},... | collective-permute-start | bytes 196616 | tf_op jit(solution)/shard_map/ppermute | solution.py:441
  61.9 1.1 collective-permute-start.12
  63.2 2.6 %collective-permute-done.14 = bf16[2,128,128]{2,1,0:T(8,128)(2,1)S(1)} collective-permute-done((bf16[2,128,128]{2,1,0:T(8,128)(2,1)}, bf16[2,128,128]{2,1,0:T(8,128)(2,1)S(1)}, u32[]{:S(2)}, u32[]{:S(2)}) %collective-permute-start.14) | collective-permute-done | bytes 65568 | tf_op jit(solution)/shard_map/ppermute | solution.py:441
  65.7 1.4 collective-permute-done.13
  67.2 0.9 pad_maximum_fusion.refs_0_
  68.1 1.1 collective-permute-start.15
  69.9 4.6 %collective-permute-done.15.refs_1_ = bf16[8,128,128]{2,1,0:T(8,128)(2,1)S(1)} collective-permute-done((bf16[8,128,128]{2,1,0:T(8,128)(2,1)S(1)}, bf16[8,128,128]{2,1,0:T(8,128)(2,1)S(1)}, u32[]{:S(2)}, u32[]{:S(2)}) %collective-permute-start.15) | collective-permute-done | bytes 262176 | tf_op jit(solution)/shard_map/ppermute | solution.py:436
  74.5 0.7 mul.378.direction
  75.3 0.7 reshape.1230.wide
  76.3 0.6 broadcast_subtract_fusion.lanes
  77.0 0.7 copy-done.4
  77.8 13.3 %take_step.1 = (f32[64,64,256]{2,1,0:T(8,128)}, f32[16,128,128]{2,1,0:T(8,128)}, f32[16,128,128]{2,1,0:T(8,128)}) custom-call(s32[1]{0:T(128)} %bitcast.6.bin_ref, f32[64]{0:T(128)} %mul.378.direction, s32[512]{0:T(512)} %copy-done.16, f32[512]{0:T(512)} %subtract_multiply_fusion.2.offset, f32[2]{0:T(128)} %sizes.3, bf16[256,64,256]{2,1,0:T(8,128)(2,1)} %dens.3, ...), custom_call_target="tpu_custom_call" | custom-call | tf_op jit(solution)/shard_map/take_step/pallas_call | solution.py:352
  91.6 2.5 %collective-permute-done.18 = f32[2,8,128,128]{3,2,1,0:T(8,128)S(1)} collective-permute-done((f32[2,8,128,128]{3,2,1,0:T(8,128)}, f32[2,8,128,128]{3,2,1,0:T(8,128)S(1)}, u32[]{:S(2)}, u32[]{:S(2)}) %collective-permute-start.18) | collective-permute-done | bytes 1048608 | tf_op jit(solution)/shard_map/ppermute | solution.py:433
  94.1 1.1 fusion
  95.2 1.7 %collective-permute-start.19 = (f32[8,128,128]{2,1,0:T(8,128)S(1)}, f32[8,128,128]{2,1,0:T(8,128)S(1)}, u32[]{:S(2)}, u32[]{:S(2)}) collective-permute-start(f32[8,128,128]{2,1,0:T(8,128)S(1)} %fusion), channel_id=1, source_target_pairs={{0,2},{1,3},{2,0},{3,1},{4,6},{5,7},{6,4},{7,5},{8,10},{9,11},{10,... | collective-permute-start | bytes 1572872 | tf_op jit(solution)/shard_map/ppermute | solution.py:436
  96.9 12.6 %collective-permute-done.19 = f32[8,128,128]{2,1,0:T(8,128)S(1)} collective-permute-done((f32[8,128,128]{2,1,0:T(8,128)S(1)}, f32[8,128,128]{2,1,0:T(8,128)S(1)}, u32[]{:S(2)}, u32[]{:S(2)}) %collective-permute-start.19) | collective-permute-done | bytes 524320 | tf_op jit(solution)/shard_map/ppermute | solution.py:436
  109.5 1.2 fusion.2
  110.7 0.7 fusion.42
  111.4 3.1 %collective-permute-start.22 = (f32[2,128,128]{2,1,0:T(8,128)S(1)}, f32[2,128,128]{2,1,0:T(8,128)S(1)}, u32[]{:S(2)}, u32[]{:S(2)}) collective-permute-start(f32[2,128,128]{2,1,0:T(8,128)S(1)} %get-tuple-element.49), channel_id=1, source_target_pairs={{0,12},{4,0},{8,4},{12,8},{1,13},{5,1},{9,5},{13,9},{2,14},{6,2},{... | collective-permute-start | bytes 393224 | tf_op jit(solution)/shard_map/ppermute | solution.py:441
  114.5 1.3 collective-permute-start.21
  115.7 2.6 %collective-permute-done.22.refs_3_ = f32[2,128,128]{2,1,0:T(8,128)S(1)} collective-permute-done((f32[2,128,128]{2,1,0:T(8,128)S(1)}, f32[2,128,128]{2,1,0:T(8,128)S(1)}, u32[]{:S(2)}, u32[]{:S(2)}) %collective-permute-start.22) | collective-permute-done | bytes 131104 | tf_op jit(solution)/shard_map/ppermute | solution.py:441
  118.3 8.7 %collective-permute-done.21.refs_2_ = f32[2,128,128]{2,1,0:T(8,128)S(1)} collective-permute-done((f32[2,128,128]{2,1,0:T(8,128)S(1)}, f32[2,128,128]{2,1,0:T(8,128)S(1)}, u32[]{:S(2)}, u32[]{:S(2)}) %collective-permute-start.21) | collective-permute-done | bytes 131104 | tf_op jit(solution)/shard_map/ppermute | solution.py:441
  127.1 0.6 copy-done.14
  127.8 2.9 %residual_field.3 = bf16[2,128,128]{2,1,0:T(8,128)(2,1)} custom-call(f32[32]{0:T(128)} %fusion.36.tally, f32[16,128,128]{2,1,0:T(8,128)} %add_negate_fusion.ctf, bf16[128,256]{1,0:T(8,128)(2,1)} %constant.239.clone.table, f32[2,128,128]{2,1,0:T(8,128)} %get-tuple-element.52.refs_0_, f32[2,128,128]{2,1,0:T(8,128)} %copy-done.15, f32[2,128,128]{2,1,0:T(8,128)} %copy-done.14, ...), custom_call_target="tpu_custom_call" | custom-call | tf_op jit(solution)/shard_map/residual_field/pallas_call | solution.py:277
  130.7 0.8 collective-permute-start.24
  131.5 3.1 %collective-permute-start.23 = (bf16[2,128,128]{2,1,0:T(8,128)(2,1)}, bf16[2,128,128]{2,1,0:T(8,128)(2,1)S(1)}, u32[]{:S(2)}, u32[]{:S(2)}) collective-permute-start(bf16[2,128,128]{2,1,0:T(8,128)(2,1)} %residual_field.3), channel_id=1, source_target_pairs={{0,12},{4,0},{8,4},{12,8},{1,13},{5,1},{9,5},{13,9},{2,14},{6,2},{... | collective-permute-start | bytes 196616 | tf_op jit(solution)/shard_map/ppermute | solution.py:441
  134.5 2.6 %collective-permute-done.25 = bf16[2,128,128]{2,1,0:T(8,128)(2,1)S(1)} collective-permute-done((bf16[2,128,128]{2,1,0:T(8,128)(2,1)}, bf16[2,128,128]{2,1,0:T(8,128)(2,1)S(1)}, u32[]{:S(2)}, u32[]{:S(2)}) %collective-permute-start.25) | collective-permute-done | bytes 65568 | tf_op jit(solution)/shard_map/ppermute | solution.py:441
  137.2 1.2 collective-permute-done.24
  138.4 0.9 pad_maximum_fusion.1.refs_0_
  139.3 0.7 collective-permute-start.26
  140.0 5.7 %collective-permute-done.26.refs_1_ = bf16[8,128,128]{2,1,0:T(8,128)(2,1)S(1)} collective-permute-done((bf16[8,128,128]{2,1,0:T(8,128)(2,1)S(1)}, bf16[8,128,128]{2,1,0:T(8,128)(2,1)S(1)}, u32[]{:S(2)}, u32[]{:S(2)}) %collective-permute-start.26) | collective-permute-done | bytes 262176 | tf_op jit(solution)/shard_map/ppermute | solution.py:436
  145.7 1.5 collective-permute-done.28.refs_3_
  147.3 0.7 copy-done.8
  148.0 9.2 %finish.1 = (f32[64,64,256]{2,1,0:T(8,128)}, f32[64,64,256]{2,1,0:T(8,128)}) custom-call(s32[512]{0:T(512)} %copy-done.16, f32[2]{0:T(128)} %sizes.3, f32[64,64,256]{2,1,0:T(8,128)} %get-tuple-element.37.first, f32[2,512]{1,0:T(2,128)} %reshape.1230.wide, f32[16,1,512]{2,1,0:T(1,128)} %broadcast_subtract_fusion.lanes, ...), custom_call_target="tpu_custom_call" | custom-call | tf_op jit(solution)/shard_map/finish/pallas_call | solution.py:399
  (142 shorter events, 9.4 us)
Async XLA Ops:
  0.6 10.1 %copy-start = (f32[4,8]{1,0:T(4,128)S(1)}, f32[4,8]{1,0:T(4,128)}, u32[]{:S(2)}) copy-start(f32[4,8]{1,0:T(4,128)} %param.17) | copy-start | bytes 388
  3.7 29.6 %collective-permute-start.2 = (s32[4]{0:T(128)S(1)}, s32[4]{0:T(128)S(1)}, u32[]{:S(2)}, u32[]{:S(2)}) collective-permute-start(s32[4]{0:T(128)S(1)} %get-tuple-element.72), channel_id=1, source_target_pairs={{0,12},{4,0},{8,4},{12,8},{1,13},{5,1},{9,5},{13,9},{2,14},{6,2},{... | collective-permute-start | bytes 56 | tf_op jit(solution)/shard_map/ppermute | solution.py:441
  8.7 26.0 %collective-permute-start.1 = (s32[4]{0:T(128)S(1)}, s32[4]{0:T(128)S(1)}, u32[]{:S(2)}, u32[]{:S(2)}) collective-permute-start(s32[4]{0:T(128)S(1)} %get-tuple-element.73), channel_id=1, source_target_pairs={{0,8},{4,12},{8,0},{12,4},{1,9},{5,13},{9,1},{13,5},{2,10},{6,14},... | collective-permute-start | bytes 56 | tf_op jit(solution)/shard_map/ppermute | solution.py:441
  8.7 26.0 %collective-permute-start = (s32[4]{0:T(128)S(1)}, s32[4]{0:T(128)S(1)}, u32[]{:S(2)}, u32[]{:S(2)}) collective-permute-start(s32[4]{0:T(128)S(1)} %get-tuple-element.74), channel_id=1, source_target_pairs={{0,4},{4,8},{8,12},{12,0},{1,5},{5,9},{9,13},{13,1},{2,6},{6,10},{... | collective-permute-start | bytes 56 | tf_op jit(solution)/shard_map/ppermute | solution.py:441
  12.7 10.4 %copy-start.17 = (s32[512]{0:T(512)}, s32[512]{0:T(512)S(1)}, u32[]{:S(2)}) copy-start(s32[512]{0:T(512)S(1)} %reshape.1245.start) | copy-start | bytes 6148
  15.1 23.4 %collective-permute-start.7 = (bf16[4,128,128]{2,1,0:T(8,128)(2,1)}, bf16[4,128,128]{2,1,0:T(8,128)(2,1)S(1)}, u32[]{:S(2)}, u32[]{:S(2)}) collective-permute-start(bf16[4,128,128]{2,1,0:T(8,128)(2,1)} %get-tuple-element.32), channel_id=1, source_target_pairs={{0,4},{4,8},{8,12},{12,0},{1,5},{5,9},{9,13},{13,1},{2,6},{6,10},{... | collective-permute-start | bytes 393224 | tf_op jit(solution)/shard_map/ppermute | solution.py:441
  17.6 21.0 %collective-permute-start.8 = (bf16[4,128,128]{2,1,0:T(8,128)(2,1)}, bf16[4,128,128]{2,1,0:T(8,128)(2,1)S(1)}, u32[]{:S(2)}, u32[]{:S(2)}) collective-permute-start(bf16[4,128,128]{2,1,0:T(8,128)(2,1)} %get-tuple-element.33), channel_id=1, source_target_pairs={{0,8},{4,12},{8,0},{12,4},{1,9},{5,13},{9,1},{13,5},{2,10},{6,14},... | collective-permute-start | bytes 393224 | tf_op jit(solution)/shard_map/ppermute | solution.py:441
  23.0 10.2 %copy-start.19 = (bf16[4,128,128]{2,1,0:T(8,128)(2,1)S(1)}, bf16[4,128,128]{2,1,0:T(8,128)(2,1)}, u32[]{:S(2)}) copy-start(bf16[4,128,128]{2,1,0:T(8,128)(2,1)} %get-tuple-element.34) | copy-start | bytes 393220
  33.2 5.4 %collective-permute-start.9 = (bf16[4,128,128]{2,1,0:T(8,128)(2,1)S(1)}, bf16[4,128,128]{2,1,0:T(8,128)(2,1)S(1)}, u32[]{:S(2)}, u32[]{:S(2)}) collective-permute-start(bf16[4,128,128]{2,1,0:T(8,128)(2,1)S(1)} %copy-done.19), channel_id=1, source_target_pairs={{0,12},{4,0},{8,4},{12,8},{1,13},{5,1},{9,5},{13,9},{2,14},{6,2},{... | collective-permute-start | bytes 393224 | tf_op jit(solution)/shard_map/ppermute | solution.py:441
  34.7 13.0 %collective-permute-start.5 = (f32[2,2,128,128]{3,2,1,0:T(8,128)}, f32[2,2,128,128]{3,2,1,0:T(8,128)S(1)}, u32[]{:S(2)}, u32[]{:S(2)}) collective-permute-start(f32[2,2,128,128]{3,2,1,0:T(8,128)} %bitcast.64), channel_id=1, source_target_pairs={{0,1},{1,0},{2,3},{3,2},{4,5},{5,4},{6,7},{7,6},{8,9},{9,8},{10,11... | collective-permute-start | bytes 786440 | tf_op jit(solution)/shard_map/ppermute | solution.py:433
  35.4 3.2 %copy-start.18 = (s32[16]{0:T(128)}, s32[16]{0:T(128)S(1)}, u32[]{:S(2)}) copy-start(s32[16]{0:T(128)S(1)} %compare_select_fusion.25.label) | copy-start | bytes 196
  35.7 1.3 collective-permute-start.3
  37.1 7.4 %collective-permute-start.4 = (f32[32]{0:T(128)S(1)}, f32[32]{0:T(128)S(1)}, u32[]{:S(2)}, u32[]{:S(2)}) collective-permute-start(f32[32]{0:T(128)S(1)} %bitcast_add_fusion), channel_id=1, source_target_pairs={{0,2},{1,3},{2,0},{3,1},{4,6},{5,7},{6,4},{7,5},{8,10},{9,11},{10,... | collective-permute-start | bytes 392 | tf_op jit(solution)/shard_map/ppermute | solution.py:436
  38.6 0.6 copy-start.9
  38.6 0.7 copy-start.10
  39.3 0.7 copy-start.11
  44.4 1.7 %collective-permute-start.10 = (f32[2,2,128,128]{3,2,1,0:T(8,128)}, f32[2,2,128,128]{3,2,1,0:T(8,128)S(1)}, u32[]{:S(2)}, u32[]{:S(2)}) collective-permute-start(f32[2,2,128,128]{3,2,1,0:T(8,128)} %bitcast.65), channel_id=1, source_target_pairs={{0,1},{1,0},{2,3},{3,2},{4,5},{5,4},{6,7},{7,6},{8,9},{9,8},{10,11... | collective-permute-start | bytes 786440 | tf_op jit(solution)/shard_map/ppermute | solution.py:433
  47.1 6.4 %collective-permute-start.11 = (f32[2,128,128]{2,1,0:T(8,128)S(1)}, f32[2,128,128]{2,1,0:T(8,128)S(1)}, u32[]{:S(2)}, u32[]{:S(2)}) collective-permute-start(f32[2,128,128]{2,1,0:T(8,128)S(1)} %fusion.3), channel_id=1, source_target_pairs={{0,2},{1,3},{2,0},{3,1},{4,6},{5,7},{6,4},{7,5},{8,10},{9,11},{10,... | collective-permute-start | bytes 393224 | tf_op jit(solution)/shard_map/ppermute | solution.py:436
  49.4 6.2 %collective-permute-start.6 = (f32[2,128,128]{2,1,0:T(8,128)S(1)}, f32[2,128,128]{2,1,0:T(8,128)S(1)}, u32[]{:S(2)}, u32[]{:S(2)}) collective-permute-start(f32[2,128,128]{2,1,0:T(8,128)S(1)} %get-tuple-element.53), channel_id=1, source_target_pairs={{0,2},{1,3},{2,0},{3,1},{4,6},{5,7},{6,4},{7,5},{8,10},{9,11},{10,... | collective-permute-start | bytes 393224 | tf_op jit(solution)/shard_map/ppermute | solution.py:436
  55.5 0.7 copy-start.12
  59.0 6.7 %collective-permute-start.14 = (bf16[2,128,128]{2,1,0:T(8,128)(2,1)}, bf16[2,128,128]{2,1,0:T(8,128)(2,1)S(1)}, u32[]{:S(2)}, u32[]{:S(2)}) collective-permute-start(bf16[2,128,128]{2,1,0:T(8,128)(2,1)} %residual_field.2), channel_id=1, source_target_pairs={{0,4},{4,8},{8,12},{12,0},{1,5},{5,9},{9,13},{13,1},{2,6},{6,10},{... | collective-permute-start | bytes 196616 | tf_op jit(solution)/shard_map/ppermute | solution.py:441
  59.6 7.6 %collective-permute-start.13 = (bf16[2,128,128]{2,1,0:T(8,128)(2,1)}, bf16[2,128,128]{2,1,0:T(8,128)(2,1)S(1)}, u32[]{:S(2)}, u32[]{:S(2)}) collective-permute-start(bf16[2,128,128]{2,1,0:T(8,128)(2,1)} %residual_field.2), channel_id=1, source_target_pairs={{0,8},{4,12},{8,0},{12,4},{1,9},{5,13},{9,1},{13,5},{2,10},{6,14},... | collective-permute-start | bytes 196616 | tf_op jit(solution)/shard_map/ppermute | solution.py:441
  61.9 5.3 %collective-permute-start.12 = (bf16[2,128,128]{2,1,0:T(8,128)(2,1)}, bf16[2,128,128]{2,1,0:T(8,128)(2,1)S(1)}, u32[]{:S(2)}, u32[]{:S(2)}) collective-permute-start(bf16[2,128,128]{2,1,0:T(8,128)(2,1)} %residual_field.2), channel_id=1, source_target_pairs={{0,12},{4,0},{8,4},{12,8},{1,13},{5,1},{9,5},{13,9},{2,14},{6,2},{... | collective-permute-start | bytes 196616 | tf_op jit(solution)/shard_map/ppermute | solution.py:441
  68.1 8.9 %copy-start.1 = (bf16[8,128,128]{2,1,0:T(8,128)(2,1)}, bf16[8,128,128]{2,1,0:T(8,128)(2,1)S(1)}, u32[]{:S(2)}) copy-start(bf16[8,128,128]{2,1,0:T(8,128)(2,1)S(1)} %pad_maximum_fusion.refs_0_) | copy-start | bytes 786436
  68.1 6.4 %collective-permute-start.15 = (bf16[8,128,128]{2,1,0:T(8,128)(2,1)S(1)}, bf16[8,128,128]{2,1,0:T(8,128)(2,1)S(1)}, u32[]{:S(2)}, u32[]{:S(2)}) collective-permute-start(bf16[8,128,128]{2,1,0:T(8,128)(2,1)S(1)} %pad_maximum_fusion.refs_0_), channel_id=1, source_target_pairs={{0,2},{1,3},{2,0},{3,1},{4,6},{5,7},{6,4},{7,5},{8,10},{9,11},{10,... | collective-permute-start | bytes 786440 | tf_op jit(solution)/shard_map/ppermute | solution.py:436
  69.3 7.7 %copy-start.16 = (s32[512]{0:T(512)}, s32[512]{0:T(512)S(1)}, u32[]{:S(2)}) copy-start(s32[512]{0:T(512)S(1)} %reshape.1239.start) | copy-start | bytes 6148
  69.9 7.0 %collective-permute-start.16 = (bf16[8,128,128]{2,1,0:T(8,128)(2,1)S(1)}, bf16[8,128,128]{2,1,0:T(8,128)(2,1)S(1)}, u32[]{:S(2)}, u32[]{:S(2)}) collective-permute-start(bf16[8,128,128]{2,1,0:T(8,128)(2,1)S(1)} %pad_maximum_fusion.refs_0_), channel_id=1, source_target_pairs={{0,1},{1,0},{2,3},{3,2},{4,5},{5,4},{6,7},{7,6},{8,9},{9,8},{10,11... | collective-permute-start | bytes 786440 | tf_op jit(solution)/shard_map/ppermute | solution.py:433
  74.5 2.5 %copy-start.3 = (bf16[8,128,128]{2,1,0:T(8,128)(2,1)}, bf16[8,128,128]{2,1,0:T(8,128)(2,1)S(1)}, u32[]{:S(2)}) copy-start(bf16[8,128,128]{2,1,0:T(8,128)(2,1)S(1)} %collective-permute-done.15.refs_1_) | copy-start | bytes 786436
  74.5 2.4 %collective-permute-start.17 = (bf16[8,128,128]{2,1,0:T(8,128)(2,1)S(1)}, bf16[8,128,128]{2,1,0:T(8,128)(2,1)S(1)}, u32[]{:S(2)}, u32[]{:S(2)}) collective-permute-start(bf16[8,128,128]{2,1,0:T(8,128)(2,1)S(1)} %collective-permute-done.15.refs_1_), channel_id=1, source_target_pairs={{0,1},{1,0},{2,3},{3,2},{4,5},{5,4},{6,7},{7,6},{8,9},{9,8},{10,11... | collective-permute-start | bytes 786440 | tf_op jit(solution)/shard_map/ppermute | solution.py:433
  77.0 0.7 copy-start.4
  77.0 0.8 copy-start.5
  91.0 3.1 %collective-permute-start.18 = (f32[2,8,128,128]{3,2,1,0:T(8,128)}, f32[2,8,128,128]{3,2,1,0:T(8,128)S(1)}, u32[]{:S(2)}, u32[]{:S(2)}) collective-permute-start(f32[2,8,128,128]{3,2,1,0:T(8,128)} %bitcast.63), channel_id=1, source_target_pairs={{0,1},{1,0},{2,3},{3,2},{4,5},{5,4},{6,7},{7,6},{8,9},{9,8},{10,11... | collective-permute-start | bytes 3145736 | tf_op jit(solution)/shard_map/ppermute | solution.py:433
  95.2 14.3 %collective-permute-start.19 = (f32[8,128,128]{2,1,0:T(8,128)S(1)}, f32[8,128,128]{2,1,0:T(8,128)S(1)}, u32[]{:S(2)}, u32[]{:S(2)}) collective-permute-start(f32[8,128,128]{2,1,0:T(8,128)S(1)} %fusion), channel_id=1, source_target_pairs={{0,2},{1,3},{2,0},{3,1},{4,6},{5,7},{6,4},{7,5},{8,10},{9,11},{10,... | collective-permute-start | bytes 1572872 | tf_op jit(solution)/shard_map/ppermute | solution.py:436
  111.4 7.0 %collective-permute-start.22 = (f32[2,128,128]{2,1,0:T(8,128)S(1)}, f32[2,128,128]{2,1,0:T(8,128)S(1)}, u32[]{:S(2)}, u32[]{:S(2)}) collective-permute-start(f32[2,128,128]{2,1,0:T(8,128)S(1)} %get-tuple-element.49), channel_id=1, source_target_pairs={{0,12},{4,0},{8,4},{12,8},{1,13},{5,1},{9,5},{13,9},{2,14},{6,2},{... | collective-permute-start | bytes 393224 | tf_op jit(solution)/shard_map/ppermute | solution.py:441
  114.5 12.6 %collective-permute-start.21 = (f32[2,128,128]{2,1,0:T(8,128)S(1)}, f32[2,128,128]{2,1,0:T(8,128)S(1)}, u32[]{:S(2)}, u32[]{:S(2)}) collective-permute-start(f32[2,128,128]{2,1,0:T(8,128)S(1)} %get-tuple-element.50), channel_id=1, source_target_pairs={{0,8},{4,12},{8,0},{12,4},{1,9},{5,13},{9,1},{13,5},{2,10},{6,14},... | collective-permute-start | bytes 393224 | tf_op jit(solution)/shard_map/ppermute | solution.py:441
  115.7 11.3 %collective-permute-start.20 = (f32[2,128,128]{2,1,0:T(8,128)S(1)}, f32[2,128,128]{2,1,0:T(8,128)S(1)}, u32[]{:S(2)}, u32[]{:S(2)}) collective-permute-start(f32[2,128,128]{2,1,0:T(8,128)S(1)} %get-tuple-element.51), channel_id=1, source_target_pairs={{0,4},{4,8},{8,12},{12,0},{1,5},{5,9},{9,13},{13,1},{2,6},{6,10},{... | collective-permute-start | bytes 393224 | tf_op jit(solution)/shard_map/ppermute | solution.py:441
  118.3 8.7 %copy-start.13 = (f32[2,128,128]{2,1,0:T(8,128)}, f32[2,128,128]{2,1,0:T(8,128)S(1)}, u32[]{:S(2)}) copy-start(f32[2,128,128]{2,1,0:T(8,128)S(1)} %collective-permute-done.22.refs_3_) | copy-start | bytes 393220
  127.1 0.6 copy-start.14
  127.1 0.7 copy-start.15
  130.7 6.5 %collective-permute-start.25 = (bf16[2,128,128]{2,1,0:T(8,128)(2,1)}, bf16[2,128,128]{2,1,0:T(8,128)(2,1)S(1)}, u32[]{:S(2)}, u32[]{:S(2)}) collective-permute-start(bf16[2,128,128]{2,1,0:T(8,128)(2,1)} %residual_field.3), channel_id=1, source_target_pairs={{0,4},{4,8},{8,12},{12,0},{1,5},{5,9},{9,13},{13,1},{2,6},{6,10},{... | collective-permute-start | bytes 196616 | tf_op jit(solution)/shard_map/ppermute | solution.py:441
  130.7 7.7 %collective-permute-start.24 = (bf16[2,128,128]{2,1,0:T(8,128)(2,1)}, bf16[2,128,128]{2,1,0:T(8,128)(2,1)S(1)}, u32[]{:S(2)}, u32[]{:S(2)}) collective-permute-start(bf16[2,128,128]{2,1,0:T(8,128)(2,1)} %residual_field.3), channel_id=1, source_target_pairs={{0,8},{4,12},{8,0},{12,4},{1,9},{5,13},{9,1},{13,5},{2,10},{6,14},... | collective-permute-start | bytes 196616 | tf_op jit(solution)/shard_map/ppermute | solution.py:441
  131.5 6.9 %collective-permute-start.23 = (bf16[2,128,128]{2,1,0:T(8,128)(2,1)}, bf16[2,128,128]{2,1,0:T(8,128)(2,1)S(1)}, u32[]{:S(2)}, u32[]{:S(2)}) collective-permute-start(bf16[2,128,128]{2,1,0:T(8,128)(2,1)} %residual_field.3), channel_id=1, source_target_pairs={{0,12},{4,0},{8,4},{12,8},{1,13},{5,1},{9,5},{13,9},{2,14},{6,2},{... | collective-permute-start | bytes 196616 | tf_op jit(solution)/shard_map/ppermute | solution.py:441
  139.3 8.0 %copy-start.2 = (bf16[8,128,128]{2,1,0:T(8,128)(2,1)}, bf16[8,128,128]{2,1,0:T(8,128)(2,1)S(1)}, u32[]{:S(2)}) copy-start(bf16[8,128,128]{2,1,0:T(8,128)(2,1)S(1)} %pad_maximum_fusion.1.refs_0_) | copy-start | bytes 786436
  139.3 6.4 %collective-permute-start.26 = (bf16[8,128,128]{2,1,0:T(8,128)(2,1)S(1)}, bf16[8,128,128]{2,1,0:T(8,128)(2,1)S(1)}, u32[]{:S(2)}, u32[]{:S(2)}) collective-permute-start(bf16[8,128,128]{2,1,0:T(8,128)(2,1)S(1)} %pad_maximum_fusion.1.refs_0_), channel_id=1, source_target_pairs={{0,2},{1,3},{2,0},{3,1},{4,6},{5,7},{6,4},{7,5},{8,10},{9,11},{10,... | collective-permute-start | bytes 786440 | tf_op jit(solution)/shard_map/ppermute | solution.py:436
  140.0 5.7 %collective-permute-start.27 = (bf16[8,128,128]{2,1,0:T(8,128)(2,1)S(1)}, bf16[8,128,128]{2,1,0:T(8,128)(2,1)S(1)}, u32[]{:S(2)}, u32[]{:S(2)}) collective-permute-start(bf16[8,128,128]{2,1,0:T(8,128)(2,1)S(1)} %pad_maximum_fusion.1.refs_0_), channel_id=1, source_target_pairs={{0,1},{1,0},{2,3},{3,2},{4,5},{5,4},{6,7},{7,6},{8,9},{9,8},{10,11... | collective-permute-start | bytes 786440 | tf_op jit(solution)/shard_map/ppermute | solution.py:433
  145.7 1.5 copy-start.6
  145.7 1.5 collective-permute-start.28
  145.7 1.5 copy-start.7
  147.3 0.7 copy-start.8

commit v3 on v2

--- a/solution.py
+++ b/solution.py
@@ -173,24 +173,50 @@
     )(*geo, density, pool_t)
 
 
-def pick_kernel(order, images, *outs):
+def pick_kernel(classes, owned, chips, where, bins_of, poses_of, classes_of, images, *refs):
+    groups = (len(refs) - 1) // 2
+    outs, labels, order = refs[:groups], refs[groups:-1], refs[-1]
     each = outs[0].shape[0]
-    for group, out in enumerate(outs):
+    here, chip, core = where[0], where[1], where[2]
+    for slot in range(groups * each):
+        order[slot] = -1
+
+    def place(n, _):
+        away = lax.rem(bins_of[n] - here + groups, groups) * each
+
+        def taken(k, rank):
+            same = lax.rem(bins_of[k] - here + groups, groups) * each == away
+            return rank + jnp.where(same, 1, 0)
+
+        order[away + lax.fori_loop(0, n, taken, 0)] = n
+        return 0
+
+    lax.fori_loop(0, images.shape[0], place, 0)
+    for group in range(groups):
         for k in range(each):
-            out[k] = images[order[group * each + k]]
-
-
-def pick_images(images, order, groups):
-    count = order.shape[0]
-    _, side, _ = images.shape
-    out = jax.ShapeDtypeStruct((count // groups, side, side), images.dtype)
+            source = order[group * each + k]
+            image = jnp.maximum(source, 0)
+            outs[group][k] = images[image]
+            pose = poses_of[image]
+            owner = pose // owned
+            ahead = lax.rem(owner // 2 - chip + chips, chips)
+            across = lax.rem(lax.rem(owner, 2) + core, 2)
+            at = (across * chips + ahead) * owned + lax.rem(pose, owned)
+            labels[group][k] = jnp.where(source >= 0, at * classes + classes_of[image], -1)
+
+
+def pick_images(images, where, image_bin, image_pose, image_class, classes, owned, chips, groups):
+    count, side, _ = images.shape
+    each = count // 4
     return pl.pallas_call(
-        pick_kernel,
-        in_specs=[smem(), vmem()],
-        out_specs=[vmem()] * groups,
-        out_shape=[out] * groups,
+        functools.partial(pick_kernel, classes, owned, chips),
+        in_specs=[smem()] * 4 + [vmem()],
+        out_specs=[vmem()] * groups + [smem()] * groups,
+        out_shape=[jax.ShapeDtypeStruct((each, side, side), images.dtype)] * groups
+        + [jax.ShapeDtypeStruct((each,), jnp.int32)] * groups,
+        scratch_shapes=[pltpu.SMEM((groups * each,), jnp.int32)],
         name="pick_images",
-    )(order, images)
+    )(where, image_bin, image_pose, image_class, images)
 
 
 def times_hartley(value, table):
@@ -424,7 +450,6 @@
     image_count, side, _ = images.shape
     pose_count = pose_offset.shape[1]
     classes = defocus.shape[0]
-    capacity = image_count // 4
     row_share = map_side // bins
     owned = pose_count // slabs
     weight = 16.0 * pose_count / (image_count * slabs)
@@ -440,6 +465,15 @@
     def to_bin(value, shift):
         return lax.ppermute(value, "bin", [(b, (b + shift) % bins) for b in range(bins)])
 
+    where = jnp.stack([bin_index, chip, core]).astype(jnp.int32)
+    picked = pick_images(
+        images, where, image_bin[:, 0], image_pose, image_class, classes, owned, chips, bins
+    )
+    picked, pose_offset, defocus = lax.optimization_barrier((picked, pose_offset, defocus))
+    marks, picked = picked[bins:], picked[:bins]
+    got_marks = [marks[0]] + [to_bin(marks[d], d) for d in range(1, bins)]
+    got_images = [picked[0]] + [to_bin(picked[d], d) for d in range(1, bins)]
+    label = jnp.concatenate(got_marks)
     cores_on, chips_on, place = jnp.meshgrid(
         jnp.arange(2), jnp.arange(chips), jnp.arange(owned), indexing="ij"
     )
@@ -467,27 +501,6 @@
     table = hartley_table(side)
     ctf = ctf_table(defocus, side)
 
-    target = image_bin[:, 0]
-    chosen = (target[:, None] == jnp.arange(bins, dtype=jnp.int32)[None, :]).astype(jnp.int32)
-    rank = jnp.sum((jnp.cumsum(chosen, axis=0) - chosen) * chosen, axis=1)
-    slot = (target - bin_index) % bins * capacity + rank
-    placement = jnp.arange(bins * capacity, dtype=jnp.int32)[:, None] == slot[None, :]
-    order = jnp.sum(
-        jnp.where(placement, jnp.arange(image_count, dtype=jnp.int32)[None, :], 0), axis=1
-    )
-    mark = image_pose * classes + image_class + 1
-    marks = jnp.sum(jnp.where(placement, mark[None, :], 0), axis=1) - 1
-    picked = pick_images(images, order, bins)
-    picked, own_geo = lax.optimization_barrier((picked, own_geo))
-    marks = marks.reshape(bins, capacity)
-    got_images = [picked[0]] + [to_bin(picked[d], d) for d in range(1, bins)]
-    got_marks = [marks[0]] + [to_bin(marks[d], d) for d in range(1, bins)]
-    got_marks = jnp.concatenate(got_marks)
-    got_pose, got_class = got_marks // classes, got_marks % classes
-    at = jnp.argmax(
-        (got_pose[:, None] == own_order[None, :]).astype(jnp.int32), axis=1
-    ).astype(jnp.int32)
-    label = jnp.where(got_marks >= 0, at * classes + got_class, -1)
     tally = jnp.sum(
         (
             label[:, None]
@@ -508,6 +521,7 @@
         return value.reshape(chips, -1, *value.shape[1:])
 
     keep, send = first_projection(density, pool_t, own_geo, pose_count)
+    keep, send, geo, wide_geo = lax.optimization_barrier((keep, send, geo, wide_geo))
     proj_parts = reduce_slab(split(keep), split(send))
     keep, send = image_sums(got_images, label, ctf, table, pose_count)
     total = functools.reduce(jnp.add, reduce_slab(split(keep), split(send)))

time: 158 us -> 159 us (level)
  waiting for transfers between devices: 51 us -> 54 us
  other arithmetic: 17.7 us -> 14.8 us
  Pallas kernels: 44.8 us -> 46.4 us
    ppermute x15, waiting for transfers between devices: 19.2 us -> 21.6 us  [to_bin(): lax.ppermute(value, 'bin', [(b, (b + shift) % bins) for b in range(bins)])]
    ppermute x6, starting transfers between devices: 7.03 us -> 8.79 us  [to_chip(): lax.ppermute(value, 'slab', [(s, (s + 2 * shift) % slabs) for s in range(...]
    unnamed x40 -> x42, local copies, waits for them, and re-layouts: 4.18 us -> 3.48 us
  transfers between devices with their start and end apart: 29 -> 29, of which waited for: 15 -> 17; matrix products, arithmetic and copies ran while one was open for 11% -> 10% of each run, Pallas kernels for 11% -> 9%
where the time goes in v3:
time: 159 us; the launch traced here: 158 us
  waiting for transfers between devices  54 us (34%)
  Pallas kernels  46.4 us (29%)
  starting transfers between devices  31.7 us (20%)
  other arithmetic  14.8 us (9%)
  local copies, waits for them, and re-layouts  10.5 us (7%)
    ppermute x6, waiting for transfers between devices, to_chip(): lax.ppermute(value, 'slab', [(s, (s + 2 * shift) % slabs) for s in range(...  26.6 us
    ppermute x15, starting transfers between devices, to_bin(): lax.ppermute(value, 'bin', [(b, (b + shift) % bins) for b in range(bins)])  22.4 us
    ppermute x15, waiting for transfers between devices, to_bin(): lax.ppermute(value, 'bin', [(b, (b + shift) % bins) for b in range(bins)])  21.6 us
    pallas_call x1, Pallas kernels, take_step(): pl.pallas_call(functools.partial(step_kernel, map_side, poses, len(fields...  13.3 us
    pallas_call x1, Pallas kernels, first_projection(): pl.pallas_call(functools.partial(first_projection_kernel, map_side, poses...  10.2 us
    pallas_call x1, Pallas kernels, finish(): pl.pallas_call(functools.partial(finish_kernel, map_side, poses, len(fiel...  9.22 us
    ppermute x6, starting transfers between devices, to_chip(): lax.ppermute(value, 'slab', [(s, (s + 2 * shift) % slabs) for s in range(...  8.79 us
    ppermute x8, waiting for transfers between devices, to_core(): return lax.ppermute(value, 'slab', [(s, s ^ 1) for s in range(slabs)])  5.79 us
  transfers between devices with their start and end apart: 29, of which 17 were waited for; matrix products, arithmetic and copies ran while one was open for 10% of the time, Pallas kernels for 9%

profile of v3, /device:TPU:0, one launch (start us, length us, event | category | flops | bytes accessed | tf_op | source)
XLA Modules:
  0.0 158.4 jit_solution(11682479384767409335)
XLA Ops:
  0.7 0.7 pad_add_fusion.where
  1.3 3.5 %pick_images.1 = (bf16[4,128,128]{2,1,0:T(8,128)(2,1)}, bf16[4,128,128]{2,1,0:T(8,128)(2,1)}, bf16[4,128,128]{2,1,0:T(8,128)(2,1)}, bf16[4,128,128]{2,1,0:T(8,12...) custom-call(s32[3]{0:T(128)} %pad_add_fusion.where, s32[16]{0:T(128)} %bitcast.62, s32[16]{0:T(128)} %poses_of.1, ...), custom_call_target="tpu_custom_call" | custom-call | tf_op jit(solution)/shard_map/pick_images/pallas_call | solution.py:211
  4.8 3.1 %collective-permute-start = (s32[4]{0:T(128)}, s32[4]{0:T(128)S(1)}, u32[]{:S(2)}, u32[]{:S(2)}) collective-permute-start(s32[4]{0:T(128)} %get-tuple-element.51), channel_id=1, source_target_pairs={{0,4},{4,8},{8,12},{12,0},{1,5},{5,9},{9,13},{13,1},{2,6},{6,10},{... | collective-permute-start | bytes 56 | tf_op jit(solution)/shard_map/ppermute | solution.py:466
  7.9 2.6 %collective-permute-start.1 = (s32[4]{0:T(128)}, s32[4]{0:T(128)S(1)}, u32[]{:S(2)}, u32[]{:S(2)}) collective-permute-start(s32[4]{0:T(128)} %get-tuple-element.52), channel_id=1, source_target_pairs={{0,8},{4,12},{8,0},{12,4},{1,9},{5,13},{9,1},{13,5},{2,10},{6,14},... | collective-permute-start | bytes 56 | tf_op jit(solution)/shard_map/ppermute | solution.py:466
  10.5 1.3 collective-permute-start.2
  11.8 0.7 collective-permute-start.7
  16.2 0.6 gather_fusion
  17.0 0.7 broadcast_multiply_fusion.4
  17.7 0.6 mul.344.direction
  18.4 0.7 mul.365.direction
  19.8 0.7 reshape.1059.wide
  20.8 0.6 subtract_multiply_fusion.1.offset
  21.4 0.6 subtract_multiply_fusion.2.offset
  22.0 0.6 broadcast_subtract_fusion.lanes
  22.7 10.2 %first_projection.1 = (f32[4,128,128]{2,1,0:T(8,128)}, f32[4,128,128]{2,1,0:T(8,128)}) custom-call(f32[16]{0:T(128)} %mul.344.direction, s32[512]{0:T(512)} %copy-done.17, f32[512]{0:T(512)} %subtract_multiply_fusion.2.offset, bf16[256,64,256]{2,1,0:T(8,128)(2,1)} %dens.3, bf16[256,128]{1,0:T(8,128)(2,1)} %constant.195.clone.pool_t), custom_call_target="tpu_custom_call" | custom-call | tf_op jit(solution)/shard_map/first_projection/pallas_call | solution.py:160
  33.0 1.6 add_negate_fusion.ctf
  34.6 2.8 %collective-permute-start.9 = (bf16[4,128,128]{2,1,0:T(8,128)(2,1)S(1)}, bf16[4,128,128]{2,1,0:T(8,128)(2,1)S(1)}, u32[]{:S(2)}, u32[]{:S(2)}) collective-permute-start(bf16[4,128,128]{2,1,0:T(8,128)(2,1)S(1)} %copy-done.20), channel_id=1, source_target_pairs={{0,12},{4,0},{8,4},{12,8},{1,13},{5,1},{9,5},{13,9},{2,14},{6,2},{... | collective-permute-start | bytes 393224 | tf_op jit(solution)/shard_map/ppermute | solution.py:466
  37.8 3.1 %collective-permute-done.9.refs_3_ = bf16[4,128,128]{2,1,0:T(8,128)(2,1)S(1)} collective-permute-done((bf16[4,128,128]{2,1,0:T(8,128)(2,1)S(1)}, bf16[4,128,128]{2,1,0:T(8,128)(2,1)S(1)}, u32[]{:S(2)}, u32[]{:S(2)}) %collective-permute-start.9) | collective-permute-done | bytes 131104 | tf_op jit(solution)/shard_map/ppermute | solution.py:466
  40.9 0.6 copy-done.11
  41.6 4.5 %image_sums.1 = (f32[4,128,128]{2,1,0:T(8,128)}, f32[4,128,128]{2,1,0:T(8,128)}) custom-call(s32[16]{0:T(128)} %copy-done.18, f32[16,128,128]{2,1,0:T(8,128)} %add_negate_fusion.ctf, bf16[128,256]{1,0:T(8,128)(2,1)} %constant.197.clone.table, bf16[4,128,128]{2,1,0:T(8,128)(2,1)} %get-tuple-element.57.refs_0_, bf16[4,128,128]{2,1,0:T(8,128)(2,1)} %copy-done.9, ...), custom_call_target="tpu_custom_call" | custom-call | tf_op jit(solution)/shard_map/image_sums/pallas_call | solution.py:265
  46.2 1.5 collective-permute-start.4
  47.9 1.9 %collective-permute-done.4 = f32[32]{0:T(128)S(1)} collective-permute-done((f32[32]{0:T(128)S(1)}, f32[32]{0:T(128)S(1)}, u32[]{:S(2)}, u32[]{:S(2)}) %collective-permute-start.4) | collective-permute-done | bytes 160 | tf_op jit(solution)/shard_map/ppermute | solution.py:461
  49.7 0.6 fusion.31.tally
  50.3 0.9 fusion.3
  51.2 1.6 collective-permute-start.11
  52.8 1.7 %fusion.6 = (f32[2,128,128]{2,1,0:T(8,128)S(1)}, f32[2,128,128]{2,1,0:T(8,128)}) fusion(f32[2,2,128,128]{3,2,1,0:T(8,128)S(1)} %collective-permute-done.5, f32[4,128,128]{2,1,0:T(8,128)} %get-tuple-element.55), kind=kLoop, calls=%fused_computation.17 | loop fusion | flops 65536 | bytes 786432 | tf_op jit(solution)/shard_map/add | solution.py:514
  55.0 1.4 collective-permute-done.11
  56.4 1.6 %fusion.5.refs_2_.refs_4_ = f32[2,128,128]{2,1,0:T(8,128)} fusion(f32[2,128,128]{2,1,0:T(8,128)S(1)} %collective-permute-done.11, f32[2,2,128,128]{3,2,1,0:T(8,128)S(1)} %collective-permute-done.10, f32[4,128,128]{2,1,0:T(8,128)} %get-tuple-element.61), kind=kLoop, calls=%fused_computation.15 | loop fusion | flops 65536 | bytes 524288 | tf_op jit(solution)/shard_map/add | solution.py:527
  58.0 1.4 collective-permute-done.6.refs_1_
  59.4 0.7 copy-done.12
  60.1 2.8 %residual_field.2 = bf16[2,128,128]{2,1,0:T(8,128)(2,1)} custom-call(f32[32]{0:T(128)} %fusion.31.tally, f32[16,128,128]{2,1,0:T(8,128)} %add_negate_fusion.ctf, bf16[128,256]{1,0:T(8,128)(2,1)} %constant.197.clone.table, f32[2,128,128]{2,1,0:T(8,128)} %get-tuple-element.75.refs_0_, f32[2,128,128]{2,1,0:T(8,128)} %copy-done.12, ...), custom_call_target="tpu_custom_call" | custom-call | tf_op jit(solution)/shard_map/residual_field/pallas_call | solution.py:303
  62.9 2.0 %collective-permute-start.14 = (bf16[2,128,128]{2,1,0:T(8,128)(2,1)}, bf16[2,128,128]{2,1,0:T(8,128)(2,1)S(1)}, u32[]{:S(2)}, u32[]{:S(2)}) collective-permute-start(bf16[2,128,128]{2,1,0:T(8,128)(2,1)} %residual_field.2), channel_id=1, source_target_pairs={{0,4},{4,8},{8,12},{12,0},{1,5},{5,9},{9,13},{13,1},{2,6},{6,10},{... | collective-permute-start | bytes 196616 | tf_op jit(solution)/shard_map/ppermute | solution.py:466
  64.9 1.8 %collective-permute-start.13 = (bf16[2,128,128]{2,1,0:T(8,128)(2,1)}, bf16[2,128,128]{2,1,0:T(8,128)(2,1)S(1)}, u32[]{:S(2)}, u32[]{:S(2)}) collective-permute-start(bf16[2,128,128]{2,1,0:T(8,128)(2,1)} %residual_field.2), channel_id=1, source_target_pairs={{0,8},{4,12},{8,0},{12,4},{1,9},{5,13},{9,1},{13,5},{2,10},{6,14},... | collective-permute-start | bytes 196616 | tf_op jit(solution)/shard_map/ppermute | solution.py:466
  66.7 0.6 collective-permute-start.12
  67.3 1.9 %collective-permute-done.14 = bf16[2,128,128]{2,1,0:T(8,128)(2,1)S(1)} collective-permute-done((bf16[2,128,128]{2,1,0:T(8,128)(2,1)}, bf16[2,128,128]{2,1,0:T(8,128)(2,1)S(1)}, u32[]{:S(2)}, u32[]{:S(2)}) %collective-permute-start.14) | collective-permute-done | bytes 65568 | tf_op jit(solution)/shard_map/ppermute | solution.py:466
  69.2 1.4 collective-permute-done.13
  70.6 0.7 collective-permute-done.12
  71.3 0.9 pad_maximum_fusion.refs_0_
  72.2 1.7 %collective-permute-start.15 = (bf16[8,128,128]{2,1,0:T(8,128)(2,1)S(1)}, bf16[8,128,128]{2,1,0:T(8,128)(2,1)S(1)}, u32[]{:S(2)}, u32[]{:S(2)}) collective-permute-start(bf16[8,128,128]{2,1,0:T(8,128)(2,1)S(1)} %pad_maximum_fusion.refs_0_), channel_id=1, source_target_pairs={{0,2},{1,3},{2,0},{3,1},{4,6},{5,7},{6,4},{7,5},{8,10},{9,11},{10,... | collective-permute-start | bytes 786440 | tf_op jit(solution)/shard_map/ppermute | solution.py:461
  73.9 4.9 %collective-permute-done.15.refs_1_ = bf16[8,128,128]{2,1,0:T(8,128)(2,1)S(1)} collective-permute-done((bf16[8,128,128]{2,1,0:T(8,128)(2,1)S(1)}, bf16[8,128,128]{2,1,0:T(8,128)(2,1)S(1)}, u32[]{:S(2)}, u32[]{:S(2)}) %collective-permute-start.15) | collective-permute-done | bytes 262176 | tf_op jit(solution)/shard_map/ppermute | solution.py:461
  78.8 1.5 collective-permute-done.17.refs_3_
  80.3 0.7 copy-done.8
  81.0 13.3 %take_step.1 = (f32[64,64,256]{2,1,0:T(8,128)}, f32[16,128,128]{2,1,0:T(8,128)}, f32[16,128,128]{2,1,0:T(8,128)}) custom-call(s32[1]{0:T(128)} %bitcast.bin_ref, f32[64]{0:T(128)} %mul.365.direction, s32[512]{0:T(512)} %copy-done.16, f32[512]{0:T(512)} %subtract_multiply_fusion.1.offset, f32[2]{0:T(128)} %sizes.3, bf16[256,64,256]{2,1,0:T(8,128)(2,1)} %dens.3, ...), custom_call_target="tpu_custom_call" | custom-call | tf_op jit(solution)/shard_map/take_step/pallas_call | solution.py:378
  94.5 2.7 %collective-permute-done.18 = f32[2,8,128,128]{3,2,1,0:T(8,128)S(1)} collective-permute-done((f32[2,8,128,128]{3,2,1,0:T(8,128)}, f32[2,8,128,128]{3,2,1,0:T(8,128)S(1)}, u32[]{:S(2)}, u32[]{:S(2)}) %collective-permute-start.18) | collective-permute-done | bytes 1048608 | tf_op jit(solution)/shard_map/ppermute | solution.py:458
  97.3 1.1 fusion
  98.4 1.8 %collective-permute-start.19 = (f32[8,128,128]{2,1,0:T(8,128)S(1)}, f32[8,128,128]{2,1,0:T(8,128)S(1)}, u32[]{:S(2)}, u32[]{:S(2)}) collective-permute-start(f32[8,128,128]{2,1,0:T(8,128)S(1)} %fusion), channel_id=1, source_target_pairs={{0,2},{1,3},{2,0},{3,1},{4,6},{5,7},{6,4},{7,5},{8,10},{9,11},{10,... | collective-permute-start | bytes 1572872 | tf_op jit(solution)/shard_map/ppermute | solution.py:461
  100.2 12.2 %collective-permute-done.19 = f32[8,128,128]{2,1,0:T(8,128)S(1)} collective-permute-done((f32[8,128,128]{2,1,0:T(8,128)S(1)}, f32[8,128,128]{2,1,0:T(8,128)S(1)}, u32[]{:S(2)}, u32[]{:S(2)}) %collective-permute-start.19) | collective-permute-done | bytes 524320 | tf_op jit(solution)/shard_map/ppermute | solution.py:461
  112.4 1.2 fusion.2
  113.6 0.7 fusion.37
  114.3 2.2 %collective-permute-start.22 = (f32[2,128,128]{2,1,0:T(8,128)S(1)}, f32[2,128,128]{2,1,0:T(8,128)S(1)}, u32[]{:S(2)}, u32[]{:S(2)}) collective-permute-start(f32[2,128,128]{2,1,0:T(8,128)S(1)} %get-tuple-element.70), channel_id=1, source_target_pairs={{0,12},{4,0},{8,4},{12,8},{1,13},{5,1},{9,5},{13,9},{2,14},{6,2},{... | collective-permute-start | bytes 393224 | tf_op jit(solution)/shard_map/ppermute | solution.py:466
  117.2 3.2 %collective-permute-done.22.refs_3_ = f32[2,128,128]{2,1,0:T(8,128)S(1)} collective-permute-done((f32[2,128,128]{2,1,0:T(8,128)S(1)}, f32[2,128,128]{2,1,0:T(8,128)S(1)}, u32[]{:S(2)}, u32[]{:S(2)}) %collective-permute-start.22) | collective-permute-done | bytes 131104 | tf_op jit(solution)/shard_map/ppermute | solution.py:466
  120.4 7.8 %collective-permute-done.21.refs_2_ = f32[2,128,128]{2,1,0:T(8,128)S(1)} collective-permute-done((f32[2,128,128]{2,1,0:T(8,128)S(1)}, f32[2,128,128]{2,1,0:T(8,128)S(1)}, u32[]{:S(2)}, u32[]{:S(2)}) %collective-permute-start.21) | collective-permute-done | bytes 131104 | tf_op jit(solution)/shard_map/ppermute | solution.py:466
  128.2 0.6 copy-done.14
  128.9 2.9 %residual_field.3 = bf16[2,128,128]{2,1,0:T(8,128)(2,1)} custom-call(f32[32]{0:T(128)} %fusion.31.tally, f32[16,128,128]{2,1,0:T(8,128)} %add_negate_fusion.ctf, bf16[128,256]{1,0:T(8,128)(2,1)} %constant.197.clone.table, f32[2,128,128]{2,1,0:T(8,128)} %get-tuple-element.73.refs_0_, f32[2,128,128]{2,1,0:T(8,128)} %copy-done.15, f32[2,128,128]{2,1,0:T(8,128)} %copy-done.14, ...), custom_call_target="tpu_custom_call" | custom-call | tf_op jit(solution)/shard_map/residual_field/pallas_call | solution.py:303
  131.8 1.4 collective-permute-start.24
  133.2 2.9 %collective-permute-start.23 = (bf16[2,128,128]{2,1,0:T(8,128)(2,1)}, bf16[2,128,128]{2,1,0:T(8,128)(2,1)S(1)}, u32[]{:S(2)}, u32[]{:S(2)}) collective-permute-start(bf16[2,128,128]{2,1,0:T(8,128)(2,1)} %residual_field.3), channel_id=1, source_target_pairs={{0,12},{4,0},{8,4},{12,8},{1,13},{5,1},{9,5},{13,9},{2,14},{6,2},{... | collective-permute-start | bytes 196616 | tf_op jit(solution)/shard_map/ppermute | solution.py:466
  136.1 2.2 %collective-permute-done.25 = bf16[2,128,128]{2,1,0:T(8,128)(2,1)S(1)} collective-permute-done((bf16[2,128,128]{2,1,0:T(8,128)(2,1)}, bf16[2,128,128]{2,1,0:T(8,128)(2,1)S(1)}, u32[]{:S(2)}, u32[]{:S(2)}) %collective-permute-start.25) | collective-permute-done | bytes 65568 | tf_op jit(solution)/shard_map/ppermute | solution.py:466
  138.3 1.2 collective-permute-done.24
  139.6 0.9 pad_maximum_fusion.1.refs_0_
  140.4 1.7 %collective-permute-start.26 = (bf16[8,128,128]{2,1,0:T(8,128)(2,1)S(1)}, bf16[8,128,128]{2,1,0:T(8,128)(2,1)S(1)}, u32[]{:S(2)}, u32[]{:S(2)}) collective-permute-start(bf16[8,128,128]{2,1,0:T(8,128)(2,1)S(1)} %pad_maximum_fusion.1.refs_0_), channel_id=1, source_target_pairs={{0,2},{1,3},{2,0},{3,1},{4,6},{5,7},{6,4},{7,5},{8,10},{9,11},{10,... | collective-permute-start | bytes 786440 | tf_op jit(solution)/shard_map/ppermute | solution.py:461
  142.1 4.8 %collective-permute-done.26.refs_1_ = bf16[8,128,128]{2,1,0:T(8,128)(2,1)S(1)} collective-permute-done((bf16[8,128,128]{2,1,0:T(8,128)(2,1)S(1)}, bf16[8,128,128]{2,1,0:T(8,128)(2,1)S(1)}, u32[]{:S(2)}, u32[]{:S(2)}) %collective-permute-start.26) | collective-permute-done | bytes 262176 | tf_op jit(solution)/shard_map/ppermute | solution.py:461
  146.9 1.5 collective-permute-done.28.refs_3_
  148.4 0.7 copy-done.7
  149.1 9.2 %finish.1 = (f32[64,64,256]{2,1,0:T(8,128)}, f32[64,64,256]{2,1,0:T(8,128)}) custom-call(s32[512]{0:T(512)} %copy-done.16, f32[2]{0:T(128)} %sizes.3, f32[64,64,256]{2,1,0:T(8,128)} %get-tuple-element.63.first, f32[2,512]{1,0:T(2,128)} %reshape.1059.wide, f32[16,1,512]{2,1,0:T(1,128)} %broadcast_subtract_fusion.lanes, ...), custom_call_target="tpu_custom_call" | custom-call | tf_op jit(solution)/shard_map/finish/pallas_call | solution.py:425
  (136 shorter events, 7.2 us)
Async XLA Ops:
  0.6 13.1 %copy-start = (f32[4,8]{1,0:T(4,128)S(1)}, f32[4,8]{1,0:T(4,128)}, u32[]{:S(2)}) copy-start(f32[4,8]{1,0:T(4,128)} %param.17) | copy-start | bytes 388
  4.8 29.8 %collective-permute-start = (s32[4]{0:T(128)}, s32[4]{0:T(128)S(1)}, u32[]{:S(2)}, u32[]{:S(2)}) collective-permute-start(s32[4]{0:T(128)} %get-tuple-element.51), channel_id=1, source_target_pairs={{0,4},{4,8},{8,12},{12,0},{1,5},{5,9},{9,13},{13,1},{2,6},{6,10},{... | collective-permute-start | bytes 56 | tf_op jit(solution)/shard_map/ppermute | solution.py:466
  7.9 29.5 %collective-permute-start.1 = (s32[4]{0:T(128)}, s32[4]{0:T(128)S(1)}, u32[]{:S(2)}, u32[]{:S(2)}) collective-permute-start(s32[4]{0:T(128)} %get-tuple-element.52), channel_id=1, source_target_pairs={{0,8},{4,12},{8,0},{12,4},{1,9},{5,13},{9,1},{13,5},{2,10},{6,14},... | collective-permute-start | bytes 56 | tf_op jit(solution)/shard_map/ppermute | solution.py:466
  10.5 26.9 %collective-permute-start.2 = (s32[4]{0:T(128)}, s32[4]{0:T(128)S(1)}, u32[]{:S(2)}, u32[]{:S(2)}) collective-permute-start(s32[4]{0:T(128)} %get-tuple-element.53), channel_id=1, source_target_pairs={{0,12},{4,0},{8,4},{12,8},{1,13},{5,1},{9,5},{13,9},{2,14},{6,2},{... | collective-permute-start | bytes 56 | tf_op jit(solution)/shard_map/ppermute | solution.py:466
  11.8 25.9 %collective-permute-start.7 = (bf16[4,128,128]{2,1,0:T(8,128)(2,1)}, bf16[4,128,128]{2,1,0:T(8,128)(2,1)S(1)}, u32[]{:S(2)}, u32[]{:S(2)}) collective-permute-start(bf16[4,128,128]{2,1,0:T(8,128)(2,1)} %get-tuple-element.58), channel_id=1, source_target_pairs={{0,4},{4,8},{8,12},{12,0},{1,5},{5,9},{9,13},{13,1},{2,6},{6,10},{... | collective-permute-start | bytes 393224 | tf_op jit(solution)/shard_map/ppermute | solution.py:466
  12.5 25.2 %collective-permute-start.8 = (bf16[4,128,128]{2,1,0:T(8,128)(2,1)}, bf16[4,128,128]{2,1,0:T(8,128)(2,1)S(1)}, u32[]{:S(2)}, u32[]{:S(2)}) collective-permute-start(bf16[4,128,128]{2,1,0:T(8,128)(2,1)} %get-tuple-element.59), channel_id=1, source_target_pairs={{0,8},{4,12},{8,0},{12,4},{1,9},{5,13},{9,1},{13,5},{2,10},{6,14},... | collective-permute-start | bytes 393224 | tf_op jit(solution)/shard_map/ppermute | solution.py:466
  19.3 13.5 %copy-start.16 = (s32[512]{0:T(512)}, s32[512]{0:T(512)S(1)}, u32[]{:S(2)}) copy-start(s32[512]{0:T(512)S(1)} %reshape.1071.start) | copy-start | bytes 6148
  19.8 2.9 %copy-start.17 = (s32[512]{0:T(512)}, s32[512]{0:T(512)S(1)}, u32[]{:S(2)}) copy-start(s32[512]{0:T(512)S(1)} %reshape.1068.start) | copy-start | bytes 6148
  22.6 11.9 %copy-start.20 = (bf16[4,128,128]{2,1,0:T(8,128)(2,1)S(1)}, bf16[4,128,128]{2,1,0:T(8,128)(2,1)}, u32[]{:S(2)}) copy-start(bf16[4,128,128]{2,1,0:T(8,128)(2,1)} %get-tuple-element.60) | copy-start | bytes 393220
  22.6 14.8 %copy-start.19 = (s32[4]{0:T(128)S(1)}, s32[4]{0:T(128)}, u32[]{:S(2)}) copy-start(s32[4]{0:T(128)} %get-tuple-element.50) | copy-start | bytes 52
  34.6 6.3 %collective-permute-start.9 = (bf16[4,128,128]{2,1,0:T(8,128)(2,1)S(1)}, bf16[4,128,128]{2,1,0:T(8,128)(2,1)S(1)}, u32[]{:S(2)}, u32[]{:S(2)}) collective-permute-start(bf16[4,128,128]{2,1,0:T(8,128)(2,1)S(1)} %copy-done.20), channel_id=1, source_target_pairs={{0,12},{4,0},{8,4},{12,8},{1,13},{5,1},{9,5},{13,9},{2,14},{6,2},{... | collective-permute-start | bytes 393224 | tf_op jit(solution)/shard_map/ppermute | solution.py:466
  37.5 3.4 %copy-start.18 = (s32[16]{0:T(128)}, s32[16]{0:T(128)S(1)}, u32[]{:S(2)}) copy-start(s32[16]{0:T(128)S(1)} %pad_add_fusion.1.label) | copy-start | bytes 196
  37.7 8.3 %collective-permute-start.3 = (f32[2,32]{1,0:T(2,128)S(1)}, f32[2,32]{1,0:T(2,128)S(1)}, u32[]{:S(2)}, u32[]{:S(2)}) collective-permute-start(f32[2,32]{1,0:T(2,128)S(1)} %squeeze.49), channel_id=1, source_target_pairs={{0,1},{1,0},{2,3},{3,2},{4,5},{5,4},{6,7},{7,6},{8,9},{9,8},{10,11... | collective-permute-start | bytes 776 | tf_op jit(solution)/shard_map/ppermute | solution.py:458
  37.7 3.2 %copy-start.9 = (bf16[4,128,128]{2,1,0:T(8,128)(2,1)}, bf16[4,128,128]{2,1,0:T(8,128)(2,1)S(1)}, u32[]{:S(2)}) copy-start(bf16[4,128,128]{2,1,0:T(8,128)(2,1)S(1)} %collective-permute-done.7.refs_1_) | copy-start | bytes 393220
  37.8 3.2 %copy-start.10 = (bf16[4,128,128]{2,1,0:T(8,128)(2,1)}, bf16[4,128,128]{2,1,0:T(8,128)(2,1)S(1)}, u32[]{:S(2)}) copy-start(bf16[4,128,128]{2,1,0:T(8,128)(2,1)S(1)} %collective-permute-done.8.refs_2_) | copy-start | bytes 393220
  40.9 0.7 copy-start.11
  46.1 4.2 %collective-permute-start.10 = (f32[2,2,128,128]{3,2,1,0:T(8,128)}, f32[2,2,128,128]{3,2,1,0:T(8,128)S(1)}, u32[]{:S(2)}, u32[]{:S(2)}) collective-permute-start(f32[2,2,128,128]{3,2,1,0:T(8,128)} %bitcast.65), channel_id=1, source_target_pairs={{0,1},{1,0},{2,3},{3,2},{4,5},{5,4},{6,7},{7,6},{8,9},{9,8},{10,11... | collective-permute-start | bytes 786440 | tf_op jit(solution)/shard_map/ppermute | solution.py:458
  46.2 3.6 %collective-permute-start.4 = (f32[32]{0:T(128)S(1)}, f32[32]{0:T(128)S(1)}, u32[]{:S(2)}, u32[]{:S(2)}) collective-permute-start(f32[32]{0:T(128)S(1)} %bitcast_add_fusion), channel_id=1, source_target_pairs={{0,2},{1,3},{2,0},{3,1},{4,6},{5,7},{6,4},{7,5},{8,10},{9,11},{10,... | collective-permute-start | bytes 392 | tf_op jit(solution)/shard_map/ppermute | solution.py:461
  47.6 5.1 %collective-permute-start.5 = (f32[2,2,128,128]{3,2,1,0:T(8,128)}, f32[2,2,128,128]{3,2,1,0:T(8,128)S(1)}, u32[]{:S(2)}, u32[]{:S(2)}) collective-permute-start(f32[2,2,128,128]{3,2,1,0:T(8,128)} %bitcast.64), channel_id=1, source_target_pairs={{0,1},{1,0},{2,3},{3,2},{4,5},{5,4},{6,7},{7,6},{8,9},{9,8},{10,11... | collective-permute-start | bytes 786440 | tf_op jit(solution)/shard_map/ppermute | solution.py:458
  51.2 5.2 %collective-permute-start.11 = (f32[2,128,128]{2,1,0:T(8,128)S(1)}, f32[2,128,128]{2,1,0:T(8,128)S(1)}, u32[]{:S(2)}, u32[]{:S(2)}) collective-permute-start(f32[2,128,128]{2,1,0:T(8,128)S(1)} %fusion.3), channel_id=1, source_target_pairs={{0,2},{1,3},{2,0},{3,1},{4,6},{5,7},{6,4},{7,5},{8,10},{9,11},{10,... | collective-permute-start | bytes 393224 | tf_op jit(solution)/shard_map/ppermute | solution.py:461
  54.4 5.0 %collective-permute-start.6 = (f32[2,128,128]{2,1,0:T(8,128)S(1)}, f32[2,128,128]{2,1,0:T(8,128)S(1)}, u32[]{:S(2)}, u32[]{:S(2)}) collective-permute-start(f32[2,128,128]{2,1,0:T(8,128)S(1)} %get-tuple-element.74), channel_id=1, source_target_pairs={{0,2},{1,3},{2,0},{3,1},{4,6},{5,7},{6,4},{7,5},{8,10},{9,11},{10,... | collective-permute-start | bytes 393224 | tf_op jit(solution)/shard_map/ppermute | solution.py:461
  59.4 0.7 copy-start.12
  62.9 6.3 %collective-permute-start.14 = (bf16[2,128,128]{2,1,0:T(8,128)(2,1)}, bf16[2,128,128]{2,1,0:T(8,128)(2,1)S(1)}, u32[]{:S(2)}, u32[]{:S(2)}) collective-permute-start(bf16[2,128,128]{2,1,0:T(8,128)(2,1)} %residual_field.2), channel_id=1, source_target_pairs={{0,4},{4,8},{8,12},{12,0},{1,5},{5,9},{9,13},{13,1},{2,6},{6,10},{... | collective-permute-start | bytes 196616 | tf_op jit(solution)/shard_map/ppermute | solution.py:466
  64.9 5.7 %collective-permute-start.13 = (bf16[2,128,128]{2,1,0:T(8,128)(2,1)}, bf16[2,128,128]{2,1,0:T(8,128)(2,1)S(1)}, u32[]{:S(2)}, u32[]{:S(2)}) collective-permute-start(bf16[2,128,128]{2,1,0:T(8,128)(2,1)} %residual_field.2), channel_id=1, source_target_pairs={{0,8},{4,12},{8,0},{12,4},{1,9},{5,13},{9,1},{13,5},{2,10},{6,14},... | collective-permute-start | bytes 196616 | tf_op jit(solution)/shard_map/ppermute | solution.py:466
  66.7 4.6 %collective-permute-start.12 = (bf16[2,128,128]{2,1,0:T(8,128)(2,1)}, bf16[2,128,128]{2,1,0:T(8,128)(2,1)S(1)}, u32[]{:S(2)}, u32[]{:S(2)}) collective-permute-start(bf16[2,128,128]{2,1,0:T(8,128)(2,1)} %residual_field.2), channel_id=1, source_target_pairs={{0,12},{4,0},{8,4},{12,8},{1,13},{5,1},{9,5},{13,9},{2,14},{6,2},{... | collective-permute-start | bytes 196616 | tf_op jit(solution)/shard_map/ppermute | solution.py:466
  72.1 8.2 %copy-start.2 = (bf16[8,128,128]{2,1,0:T(8,128)(2,1)}, bf16[8,128,128]{2,1,0:T(8,128)(2,1)S(1)}, u32[]{:S(2)}) copy-start(bf16[8,128,128]{2,1,0:T(8,128)(2,1)S(1)} %pad_maximum_fusion.refs_0_) | copy-start | bytes 786436
  72.2 6.6 %collective-permute-start.15 = (bf16[8,128,128]{2,1,0:T(8,128)(2,1)S(1)}, bf16[8,128,128]{2,1,0:T(8,128)(2,1)S(1)}, u32[]{:S(2)}, u32[]{:S(2)}) collective-permute-start(bf16[8,128,128]{2,1,0:T(8,128)(2,1)S(1)} %pad_maximum_fusion.refs_0_), channel_id=1, source_target_pairs={{0,2},{1,3},{2,0},{3,1},{4,6},{5,7},{6,4},{7,5},{8,10},{9,11},{10,... | collective-permute-start | bytes 786440 | tf_op jit(solution)/shard_map/ppermute | solution.py:461
  73.9 4.9 %collective-permute-start.16 = (bf16[8,128,128]{2,1,0:T(8,128)(2,1)S(1)}, bf16[8,128,128]{2,1,0:T(8,128)(2,1)S(1)}, u32[]{:S(2)}, u32[]{:S(2)}) collective-permute-start(bf16[8,128,128]{2,1,0:T(8,128)(2,1)S(1)} %pad_maximum_fusion.refs_0_), channel_id=1, source_target_pairs={{0,1},{1,0},{2,3},{3,2},{4,5},{5,4},{6,7},{7,6},{8,9},{9,8},{10,11... | collective-permute-start | bytes 786440 | tf_op jit(solution)/shard_map/ppermute | solution.py:458
  78.8 1.5 copy-start.4
  78.8 1.5 collective-permute-start.17
  78.8 1.5 copy-start.6
  80.3 0.7 copy-start.8
  94.3 2.9 %collective-permute-start.18 = (f32[2,8,128,128]{3,2,1,0:T(8,128)}, f32[2,8,128,128]{3,2,1,0:T(8,128)S(1)}, u32[]{:S(2)}, u32[]{:S(2)}) collective-permute-start(f32[2,8,128,128]{3,2,1,0:T(8,128)} %bitcast.63), channel_id=1, source_target_pairs={{0,1},{1,0},{2,3},{3,2},{4,5},{5,4},{6,7},{7,6},{8,9},{9,8},{10,11... | collective-permute-start | bytes 3145736 | tf_op jit(solution)/shard_map/ppermute | solution.py:458
  98.4 14.0 %collective-permute-start.19 = (f32[8,128,128]{2,1,0:T(8,128)S(1)}, f32[8,128,128]{2,1,0:T(8,128)S(1)}, u32[]{:S(2)}, u32[]{:S(2)}) collective-permute-start(f32[8,128,128]{2,1,0:T(8,128)S(1)} %fusion), channel_id=1, source_target_pairs={{0,2},{1,3},{2,0},{3,1},{4,6},{5,7},{6,4},{7,5},{8,10},{9,11},{10,... | collective-permute-start | bytes 1572872 | tf_op jit(solution)/shard_map/ppermute | solution.py:461
  114.3 6.1 %collective-permute-start.22 = (f32[2,128,128]{2,1,0:T(8,128)S(1)}, f32[2,128,128]{2,1,0:T(8,128)S(1)}, u32[]{:S(2)}, u32[]{:S(2)}) collective-permute-start(f32[2,128,128]{2,1,0:T(8,128)S(1)} %get-tuple-element.70), channel_id=1, source_target_pairs={{0,12},{4,0},{8,4},{12,8},{1,13},{5,1},{9,5},{13,9},{2,14},{6,2},{... | collective-permute-start | bytes 393224 | tf_op jit(solution)/shard_map/ppermute | solution.py:466
  116.5 11.7 %collective-permute-start.21 = (f32[2,128,128]{2,1,0:T(8,128)S(1)}, f32[2,128,128]{2,1,0:T(8,128)S(1)}, u32[]{:S(2)}, u32[]{:S(2)}) collective-permute-start(f32[2,128,128]{2,1,0:T(8,128)S(1)} %get-tuple-element.71), channel_id=1, source_target_pairs={{0,8},{4,12},{8,0},{12,4},{1,9},{5,13},{9,1},{13,5},{2,10},{6,14},... | collective-permute-start | bytes 393224 | tf_op jit(solution)/shard_map/ppermute | solution.py:466
  117.0 11.2 %collective-permute-start.20 = (f32[2,128,128]{2,1,0:T(8,128)S(1)}, f32[2,128,128]{2,1,0:T(8,128)S(1)}, u32[]{:S(2)}, u32[]{:S(2)}) collective-permute-start(f32[2,128,128]{2,1,0:T(8,128)S(1)} %get-tuple-element.72), channel_id=1, source_target_pairs={{0,4},{4,8},{8,12},{12,0},{1,5},{5,9},{9,13},{13,1},{2,6},{6,10},{... | collective-permute-start | bytes 393224 | tf_op jit(solution)/shard_map/ppermute | solution.py:466
  120.4 7.8 %copy-start.13 = (f32[2,128,128]{2,1,0:T(8,128)}, f32[2,128,128]{2,1,0:T(8,128)S(1)}, u32[]{:S(2)}) copy-start(f32[2,128,128]{2,1,0:T(8,128)S(1)} %collective-permute-done.22.refs_3_) | copy-start | bytes 393220
  128.2 0.7 copy-start.14
  128.2 0.7 copy-start.15
  131.8 6.5 %collective-permute-start.25 = (bf16[2,128,128]{2,1,0:T(8,128)(2,1)}, bf16[2,128,128]{2,1,0:T(8,128)(2,1)S(1)}, u32[]{:S(2)}, u32[]{:S(2)}) collective-permute-start(bf16[2,128,128]{2,1,0:T(8,128)(2,1)} %residual_field.3), channel_id=1, source_target_pairs={{0,4},{4,8},{8,12},{12,0},{1,5},{5,9},{9,13},{13,1},{2,6},{6,10},{... | collective-permute-start | bytes 196616 | tf_op jit(solution)/shard_map/ppermute | solution.py:466
  131.8 7.7 %collective-permute-start.24 = (bf16[2,128,128]{2,1,0:T(8,128)(2,1)}, bf16[2,128,128]{2,1,0:T(8,128)(2,1)S(1)}, u32[]{:S(2)}, u32[]{:S(2)}) collective-permute-start(bf16[2,128,128]{2,1,0:T(8,128)(2,1)} %residual_field.3), channel_id=1, source_target_pairs={{0,8},{4,12},{8,0},{12,4},{1,9},{5,13},{9,1},{13,5},{2,10},{6,14},... | collective-permute-start | bytes 196616 | tf_op jit(solution)/shard_map/ppermute | solution.py:466
  133.2 6.3 %collective-permute-start.23 = (bf16[2,128,128]{2,1,0:T(8,128)(2,1)}, bf16[2,128,128]{2,1,0:T(8,128)(2,1)S(1)}, u32[]{:S(2)}, u32[]{:S(2)}) collective-permute-start(bf16[2,128,128]{2,1,0:T(8,128)(2,1)} %residual_field.3), channel_id=1, source_target_pairs={{0,12},{4,0},{8,4},{12,8},{1,13},{5,1},{9,5},{13,9},{2,14},{6,2},{... | collective-permute-start | bytes 196616 | tf_op jit(solution)/shard_map/ppermute | solution.py:466
  140.4 8.0 %copy-start.1 = (bf16[8,128,128]{2,1,0:T(8,128)(2,1)}, bf16[8,128,128]{2,1,0:T(8,128)(2,1)S(1)}, u32[]{:S(2)}) copy-start(bf16[8,128,128]{2,1,0:T(8,128)(2,1)S(1)} %pad_maximum_fusion.1.refs_0_) | copy-start | bytes 786436
  140.4 6.4 %collective-permute-start.26 = (bf16[8,128,128]{2,1,0:T(8,128)(2,1)S(1)}, bf16[8,128,128]{2,1,0:T(8,128)(2,1)S(1)}, u32[]{:S(2)}, u32[]{:S(2)}) collective-permute-start(bf16[8,128,128]{2,1,0:T(8,128)(2,1)S(1)} %pad_maximum_fusion.1.refs_0_), channel_id=1, source_target_pairs={{0,2},{1,3},{2,0},{3,1},{4,6},{5,7},{6,4},{7,5},{8,10},{9,11},{10,... | collective-permute-start | bytes 786440 | tf_op jit(solution)/shard_map/ppermute | solution.py:461
  142.1 4.8 %collective-permute-start.27 = (bf16[8,128,128]{2,1,0:T(8,128)(2,1)S(1)}, bf16[8,128,128]{2,1,0:T(8,128)(2,1)S(1)}, u32[]{:S(2)}, u32[]{:S(2)}) collective-permute-start(bf16[8,128,128]{2,1,0:T(8,128)(2,1)S(1)} %pad_maximum_fusion.1.refs_0_), channel_id=1, source_target_pairs={{0,1},{1,0},{2,3},{3,2},{4,5},{5,4},{6,7},{7,6},{8,9},{9,8},{10,11... | collective-permute-start | bytes 786440 | tf_op jit(solution)/shard_map/ppermute | solution.py:458
  146.9 1.5 copy-start.3
  146.9 1.5 collective-permute-start.28
  146.9 1.5 copy-start.5
  148.4 0.7 copy-start.7
